TPU v7x, 32 devices: a whole 2x2x4 slice. The times are simulated.
32 devices in a mesh: group: 2 (over y), expert: 4 (over z), tensor: 4 (over x, core).
Axes of the slice: x: 2, y: 2, z: 4, core: 2. Of those that a mesh axis runs over, the one named last changes fastest.
Arguments:
- q_absorbed: bfloat16 [1024, 36864], P(('group', 'expert'), 'tensor'), parts along dimension 0, may hold values from -14 to 14
- kv_latent: bfloat16 [1024, 576], P(('group', 'expert')), parts along dimension 0, may hold values from -4 to 4
- w_values: bfloat16 [64, 512, 128], P('tensor'), may hold values from -1 to 1
- w_out: bfloat16 [8192, 7168], P('tensor', 'expert'), may hold values from -0.0625 to 0.0625
- layer_input: bfloat16 [1024, 7168], P(('group', 'expert')), parts along dimension 0, may hold values from -40 to 40
- norm_gain: float32 [7168], replicated, may hold values from 0.1 to 1.9
- predicted: int32 [1024, 8], P(('group', 'expert')), parts along dimension 0, may hold values from 0 to 15, as said below
- actual: int32 [1024, 8], P(('group', 'expert')), parts along dimension 0, may hold values from 0 to 15, as said below
- gates: float32 [1024, 8], P(('group', 'expert')), parts along dimension 0, may hold values from 0.1 to 1
- w_gate: bfloat16 [16, 7168, 1024], P('expert', 'tensor'), may hold values from -0.0625 to 0.0625
- w_up: bfloat16 [16, 7168, 1024], P('expert', 'tensor'), may hold values from -0.0625 to 0.0625
- w_down: bfloat16 [16, 1024, 7168], P('expert', None, 'tensor'), may hold values from -0.1875 to 0.1875
Outputs:
- attended: bfloat16 [1024, 7168], P(('group', 'expert'), 'tensor'), parts along dimension 0
- mixture: bfloat16 [1024, 7168], P(('group', 'expert'), 'tensor'), parts along dimension 0
- missed: float32 [1024], P(('group', 'expert')), parts along dimension 0
There are 2 independent parts, one for each index of `group`. A program takes and returns all parts, laid end to end along the dimension named above; an argument that names none is the same for every part. Nothing has to cross between parts.
Inputs may be any that keep to these rules, and one draw needn't show every extreme that they name: `predicted`: each row names 8 different experts. In each aligned block of 128 rows (the rows of one index of expert) at most 80 rows name the same expert, and in every draw some expert is named by exactly 80 rows of every block. `actual`: each row names 8 different experts. In each aligned block of 128 rows (the rows of one index of expert) at most 12 rows name a given expert that the same row of predicted does not name, and in every draw some expert reaches 12 such rows in every block.
All inputs are finite; a program needn't handle non-finite values.
Results may differ from a plain program's by a relative error of at most 0.023.
Values may be sent and summed in bfloat16 or wider, within the bound.
No kernel may reach another device: no remote copies, remote signals or barrier semaphores. Data moves between devices by JAX's collectives and lax.ppermute only.
A program may use at most 128 MiB of HBM per device.

v0:
```python
import functools

import jax
import jax.numpy as jnp
from jax import lax
from jax.experimental import pallas as pl
from jax.experimental.pallas import tpu as pltpu
from jax.sharding import PartitionSpec as P


GROUP, EXPERT, TENSOR = "group", "expert", "tensor"
ROPE = 64
VDIM = 128
LANES = 128

EPS = 1e-06
FLOOR = -1e30


def line_send(value, axis, size, step):
    pairs = [(i, i + step) for i in range(size) if 0 <= i + step < size]
    return lax.ppermute(value, axis, pairs)


def line_gather(value, axis, size):
    me = lax.axis_index(axis)
    rights, lefts = [value], [value]
    for _ in range(1, size):
        rights.append(line_send(rights[-1], axis, size, 1))
        lefts.append(line_send(lefts[-1], axis, size, -1))
    return [value] + [jnp.where(me >= s, rights[s], lefts[size - s]) for s in range(1, size)]


def add(first, second):
    return (first.astype(jnp.float32) + second.astype(jnp.float32)).astype(first.dtype)


def line_scatter(blocks, axis, size):
    right, left = None, None
    for far in range(size - 1, 0, -1):
        out_right, out_left = blocks[size - far], blocks[far]
        if right is not None:
            out_right, out_left = add(out_right, right), add(out_left, left)
        right = line_send(out_right, axis, size, 1)
        left = line_send(out_left, axis, size, -1)
    return (
        blocks[0].astype(jnp.float32) + right.astype(jnp.float32) + left.astype(jnp.float32)
    ).astype(blocks[0].dtype)


def flip(value, axis, size, bit):
    return lax.ppermute(value, axis, [(i, i ^ bit) for i in range(size)])


def halve(value, axis, size, dim):
    me = lax.axis_index(axis)
    bit = 1
    while bit < size:
        half = value.shape[dim] // 2
        low = lax.slice_in_dim(value, 0, half, axis=dim)
        high = lax.slice_in_dim(value, half, 2 * half, axis=dim)
        mine = (me & bit) == 0
        got = flip(jnp.where(mine, high, low), axis, size, bit)
        value = jnp.where(mine, low, high).astype(jnp.float32) + got.astype(jnp.float32)
        bit *= 2
        if bit < size:
            value = value.astype(got.dtype)
    return value


def unhalve(value, axis, size, dim):
    me = lax.axis_index(axis)
    bit = size // 2
    while bit >= 1:
        got = flip(value, axis, size, bit)
        mine = (me & bit) == 0
        value = jnp.concatenate(
            [jnp.where(mine, value, got), jnp.where(mine, got, value)], axis=dim
        )
        bit //= 2
    return value


def attend(q_absorbed, blocks, w_values):
    token_count = q_absorbed.shape[0]
    heads_here, latent_width, _ = w_values.shape
    key_width = blocks[0].shape[1]
    scale = (VDIM + ROPE) ** (-0.5)
    me = lax.axis_index(EXPERT)
    keys = jnp.concatenate(blocks, axis=0)
    queries = q_absorbed.reshape(token_count * heads_here, key_width)
    query_pos = jnp.repeat(jnp.arange(token_count, dtype=jnp.int32), heads_here)
    index = jnp.arange(keys.shape[0], dtype=jnp.int32)
    back, place = index // token_count, index % token_count
    own = (back[None, :] == 0) & (query_pos[:, None] >= place[None, :])
    visible = own | ((back >= 1) & (back <= me))[None, :]
    scores = (
        lax.dot_general(
            queries, keys, (((1,), (1,)), ((), ())), preferred_element_type=jnp.float32
        )
        * scale
    )
    masked = jnp.where(visible, scores, FLOOR)
    largest = jnp.max(masked, axis=1)
    expo = jnp.where(visible, jnp.exp(masked - largest[:, None]), 0.0)
    denominator = jnp.sum(expo, axis=1)
    accum = jnp.dot(
        expo.astype(jnp.bfloat16), keys[:, :latent_width], preferred_element_type=jnp.float32
    )
    latent = (
        (accum / denominator[:, None])
        .astype(jnp.bfloat16)
        .reshape(token_count, heads_here, latent_width)
    )
    heads_out = jnp.einsum(
        "thc,hcv->thv", latent, w_values, preferred_element_type=jnp.float32
    ).astype(jnp.bfloat16)
    return heads_out.reshape(token_count, heads_here * w_values.shape[2])


def project(heads_out, w_out, experts, tensors):
    token_count = heads_out.shape[0]
    slots = jnp.concatenate(line_gather(heads_out, EXPERT, experts), axis=0)
    partial = jnp.dot(slots, w_out, preferred_element_type=jnp.float32).astype(jnp.bfloat16)
    if experts == tensors:
        mine = halve(partial, TENSOR, tensors, 0).astype(jnp.bfloat16)
        bits = tensors.bit_length() - 1
        pairs = []
        for e in range(experts):
            for t in range(tensors):
                slot = int(format(t, "0%db" % bits)[::-1], 2)
                pairs.append((e * tensors + t, (e - slot) % experts * tensors + e))
        return lax.ppermute(mine, (EXPERT, TENSOR), pairs)
    me = lax.axis_index(EXPERT)
    order = (me - jnp.arange(experts)) % experts
    blocks = partial.reshape(experts, token_count, -1)[order].reshape(partial.shape)
    rows = lax.all_to_all(blocks, EXPERT, split_axis=0, concat_axis=1, tiled=True)
    return lax.psum_scatter(rows, TENSOR, scatter_dimension=1, tiled=True)


def expert_rows(layer_input, norm_gain, actual, gates, slice_width, active):
    token_count = layer_input.shape[0]
    first_col = lax.axis_index(TENSOR) * slice_width
    features = layer_input.astype(jnp.float32)
    inverse = lax.rsqrt(jnp.mean(features * features, axis=1, keepdims=True) + EPS)
    mine = lax.dynamic_slice_in_dim(layer_input, first_col, slice_width, 1).astype(jnp.float32)
    gain_mine = lax.dynamic_slice_in_dim(norm_gain, first_col, slice_width, 0)
    normed = (mine * inverse * gain_mine).astype(jnp.bfloat16)
    ids = jnp.arange(active, dtype=jnp.int32)
    dense = jnp.sum(
        jnp.where(actual[:, :, None] == ids[None, None, :], gates[:, :, None], 0.0), axis=1
    )
    high = dense.astype(jnp.bfloat16)
    low = (dense - high.astype(jnp.float32)).astype(jnp.bfloat16)
    width = -(-2 * active // LANES) * LANES
    filler = jnp.zeros((token_count, width - 2 * active), jnp.bfloat16)
    return jnp.concatenate([normed, high, low, filler], axis=1)


def mix(layer_input, norm_gain, actual, gates, w_gate, w_up, w_down, experts, tensors):
    token_count = layer_input.shape[0]
    local, slice_width, hidden = w_gate.shape
    active = local * experts
    me = lax.axis_index(EXPERT)
    rows = expert_rows(layer_input, norm_gain, actual, gates, slice_width, active)
    slots = jnp.concatenate(line_gather(rows, EXPERT, experts), axis=0)
    tokens = slots[:, :slice_width]
    both = slots[:, slice_width : slice_width + 2 * active].astype(jnp.float32)
    weight = both[:, :active] + both[:, active:]
    weight = lax.dynamic_slice_in_dim(weight, me * local, local, 1)
    acts = []
    for e in range(local):
        gate_part = jnp.dot(tokens, w_gate[e], preferred_element_type=jnp.float32)
        up_part = jnp.dot(tokens, w_up[e], preferred_element_type=jnp.float32)
        pair = jnp.stack([gate_part.astype(jnp.bfloat16), up_part.astype(jnp.bfloat16)])
        share = halve(pair, TENSOR, tensors, 2)
        act = jax.nn.silu(share[0]) * share[1] * weight[:, e : e + 1]
        acts.append(unhalve(act.astype(jnp.bfloat16), TENSOR, tensors, 1))
    acts = jnp.concatenate(acts, axis=1)
    partial = jnp.dot(
        acts, w_down.reshape(local * hidden, -1), preferred_element_type=jnp.float32
    ).astype(jnp.bfloat16)
    blocks = partial.reshape(experts, token_count, -1)
    return line_scatter([blocks[s] for s in range(experts)], EXPERT, experts)


def after(value, *others):
    return lax.optimization_barrier((value, others))[0]


LINE = 4
VMEM = 10 * 1024 * 1024
OUTER = [(0, 1), (1, 0), (2, 3), (3, 2)]
INNER = [(1, 2), (2, 1)]
OUTWARD = [(1, 0), (2, 3)]
INWARD = [(0, 1), (3, 2)]


def block_at(device, slot):
    far = 2 if device < 2 else 0
    inner, outer = (2, 3) if far == 2 else (1, 0)
    return (device, device ^ 1, inner, outer)[slot]


def attention_kernel(flags, q_ref, even_ref, odd_ref, values_ref, out_ref, shut, *, scale):
    rows, keys = shut.shape
    heads = values_ref.shape[0]
    latent_width = values_ref.shape[1]
    value_width = values_ref.shape[2]
    width = q_ref.shape[1] // heads
    reach = even_ref.shape[1]

    @pl.when(pl.program_id(0) == 0)
    def _():
        query = lax.broadcasted_iota(jnp.int32, (rows, keys), 0)
        key = lax.broadcasted_iota(jnp.int32, (rows, keys), 1)
        open_to = jnp.where(key < rows, query, -1)
        for slot in range(1, keys // rows):
            other = flags[3] ^ slot
            limit = jnp.where(other < flags[3], keys, -1)
            open_to = jnp.where((key >= slot * rows) & (key < (slot + 1) * rows), limit, open_to)
        shut[...] = jnp.where(key <= open_to, 0.0, FLOOR)

    even = [q_ref[:, h * width : h * width + reach] for h in range(0, heads, 2)]
    odd = [q_ref[:, (h + 1) * width - reach : (h + 1) * width] for h in range(1, heads, 2)]
    for parity, group, key_ref in ((0, even, even_ref), (1, odd, odd_ref)):
        queries = jnp.concatenate(group, axis=0)
        scores = lax.dot_general(
            queries, key_ref[...], (((1,), (1,)), ((), ())), preferred_element_type=jnp.float32
        )
        scores = (scores * scale).reshape(len(group), rows, keys) + shut[...][None]
        largest = jnp.max(scores, axis=2, keepdims=True)
        expo = jnp.exp(scores - largest)
        bottom = jnp.sum(expo, axis=2, keepdims=True)
        total = jnp.dot(
            expo.astype(jnp.bfloat16).reshape(len(group) * rows, keys),
            even_ref[:, :latent_width],
            preferred_element_type=jnp.float32,
        ).reshape(len(group), rows, latent_width)
        latent = (total / bottom).astype(jnp.bfloat16)
        for index in range(len(group)):
            head = 2 * index + parity
            out_ref[:, head * value_width : (head + 1) * value_width] = jnp.dot(
                latent[index], values_ref[head], preferred_element_type=jnp.float32
            ).astype(out_ref.dtype)


HEADS_AT_ONCE = 4


def attention(q_absorbed, blocks, w_values, flags):
    rows = q_absorbed.shape[0]
    heads, latent_width, value_width = w_values.shape
    width = q_absorbed.shape[1] // heads
    keys = jnp.concatenate(blocks, axis=0)
    count, reach = keys.shape
    odd = jnp.concatenate(
        [jnp.zeros((count, reach - width), keys.dtype), keys[:, :width]], axis=1
    )
    group = HEADS_AT_ONCE
    flops = 2 * rows * count * (width + latent_width) * heads
    flops += 2 * rows * latent_width * value_width * heads
    return pl.pallas_call(
        functools.partial(attention_kernel, scale=(VDIM + ROPE) ** (-0.5)),
        out_shape=jax.ShapeDtypeStruct((rows, heads * value_width), jnp.bfloat16),
        grid_spec=pltpu.PrefetchScalarGridSpec(
            num_scalar_prefetch=1,
            grid=(heads // group,),
            in_specs=[
                pl.BlockSpec((rows, group * width), lambda h, flags: (0, h)),
                pl.BlockSpec((count, reach), lambda h, flags: (0, 0)),
                pl.BlockSpec((count, reach), lambda h, flags: (0, 0)),
                pl.BlockSpec((group, latent_width, value_width), lambda h, flags: (h, 0, 0)),
            ],
            out_specs=pl.BlockSpec((rows, group * value_width), lambda h, flags: (0, h)),
            scratch_shapes=[pltpu.VMEM((rows, count), jnp.float32)],
        ),
        cost_estimate=pl.CostEstimate(
            flops=flops,
            bytes_accessed=2 * rows * heads * width,
            transcendentals=rows * heads * count,
        ),
        compiler_params=pltpu.CompilerParams(vmem_limit_bytes=VMEM),
        name="attention",
    )(flags, q_absorbed, keys, odd, w_values)


def key_blocks(kv_latent, first_core):
    rows, width = kv_latent.shape
    half = rows // 2
    whole = jnp.pad(kv_latent, ((0, 0), (0, -width % LANES)))
    mine = jnp.where(first_core, whole[:half], whole[half:])
    got = []
    for step in range(1, LINE):
        got.append(flip(mine, EXPERT, LINE, step))
    got = jnp.stack(got)
    other = flip(got, TENSOR, LINE, 1)
    full = jnp.concatenate(
        [jnp.where(first_core, got, other), jnp.where(first_core, other, got)], axis=1
    )
    return [whole] + [full[index] for index in range(LINE - 1)]


def rows_kernel(flags, *refs, parts, rows, first):
    part_refs, (gate_ref, up_ref, send_ref, keep_ref, tokens) = refs[:parts], refs[parts:]
    item, side = pl.program_id(0), pl.program_id(1)

    @pl.when((item == 0) & (side == 0))
    def _():
        if parts == 2:
            tokens[:rows] = part_refs[0][...]
            tokens[rows:] = part_refs[1][...]
        else:

            @pl.when(flags[2] == 1)
            def _():
                tokens[:rows] = part_refs[0][...]
                tokens[rows:] = part_refs[1][...]

            @pl.when(flags[2] == 0)
            def _():
                tokens[:rows] = part_refs[2][...]
                tokens[rows:] = part_refs[3][...]

    def both(out_ref, core):
        half = gate_ref.shape[2] // 2
        span = pl.ds(pl.multiple_of(core * half, half), half)
        for index, weight_ref in enumerate((gate_ref, up_ref)):
            out_ref[index, 0] = jnp.dot(
                tokens[...], weight_ref[first + item, :, span], preferred_element_type=jnp.float32
            ).astype(out_ref.dtype)

    @pl.when(side == 0)
    def _():
        both(send_ref, 1 - flags[0])

    @pl.when(side == 1)
    def _():
        both(keep_ref, flags[0])


def stage_kernel(*refs):
    half = len(refs) // 2
    sources, targets, sems = refs[:half], refs[half : 2 * half], refs[-1]
    copies = []
    for which in range(half):
        for item in range(sources[which].shape[0]):
            copies.append(
                pltpu.make_async_copy(
                    sources[which].at[item], targets[which].at[item], sems.at[which, item]
                )
            )
    for copy in copies:
        copy.start()
    for copy in copies:
        copy.wait()


def stage(*weights):
    return pl.pallas_call(
        stage_kernel,
        out_shape=tuple(pltpu.VMEM(weight.shape, weight.dtype) for weight in weights),
        in_specs=[pl.BlockSpec(memory_space=pltpu.HBM)] * len(weights),
        out_specs=(pl.BlockSpec(memory_space=pltpu.VMEM),) * len(weights),
        scratch_shapes=[pltpu.SemaphoreType.DMA((len(weights), weights[0].shape[0]))],
        cost_estimate=pl.CostEstimate(
            flops=0, bytes_accessed=2 * sum(weight.size for weight in weights), transcendentals=0
        ),
        compiler_params=pltpu.CompilerParams(vmem_limit_bytes=1024 * 1024),
        name="stage",
    )(*weights)


def gate_up(parts, flags, w_gate, w_up, first, count):
    rows = parts[0].shape[0]
    _, depth, hidden = w_gate.shape
    half = hidden // 2
    out_spec = pl.BlockSpec((2, 1, 2 * rows, half), lambda e, j, flags: (0, e, 0, 0))
    out = jax.ShapeDtypeStruct((2, count, 2 * rows, half), jnp.bfloat16)
    return pl.pallas_call(
        functools.partial(rows_kernel, parts=len(parts), rows=rows, first=first),
        out_shape=(out, out),
        grid_spec=pltpu.PrefetchScalarGridSpec(
            num_scalar_prefetch=1,
            grid=(count, 2),
            in_specs=[pl.BlockSpec((rows, depth), lambda e, j, flags: (0, 0))] * len(parts)
            + [pl.BlockSpec(memory_space=pltpu.VMEM)] * 2,
            out_specs=(out_spec, out_spec),
            scratch_shapes=[pltpu.VMEM((2 * rows, depth), jnp.bfloat16)],
        ),
        cost_estimate=pl.CostEstimate(
            flops=8 * rows * depth * hidden * count,
            bytes_accessed=4 * depth * hidden * count,
            transcendentals=0,
        ),
        compiler_params=pltpu.CompilerParams(vmem_limit_bytes=VMEM),
        name="gate_up",
    )(flags, *parts, w_gate, w_up)


def down_kernel(flags, *refs, counts, rows):
    pieces, (weight_ref, low_ref, high_ref, acts) = refs[: 2 * len(counts)], refs[2 * len(counts) :]
    quarter = pieces[0].shape[3]

    @pl.when(pl.program_id(0) == 0)
    def _():
        first = 0
        for index, count in enumerate(counts):
            for item in range(count):
                for core in range(2):
                    for chip in range(2):
                        column = (first + item) * 4 + 2 * core + chip
                        span = slice(column * quarter, (column + 1) * quarter)
                        here, there = pieces[2 * index], pieces[2 * index + 1]
                        slot = flags[1] if chip == 0 else 1 - flags[1]

                        @pl.when(flags[0] == core)
                        def _(here=here, span=span, slot=slot, item=item):
                            acts[:, span] = here[slot, item]

                        @pl.when(flags[0] != core)
                        def _(there=there, span=span, slot=slot, item=item):
                            acts[:, span] = there[slot, item]

            first += count

    depth = weight_ref.shape[0] * weight_ref.shape[1]
    tile = low_ref.shape[1]
    span = pl.ds(pl.multiple_of(pl.program_id(0) * tile, tile), tile)
    total = jnp.dot(
        acts[...],
        weight_ref[:, :, span].reshape(depth, tile),
        preferred_element_type=jnp.float32,
    )
    low_ref[...] = total[:rows].astype(low_ref.dtype)
    high_ref[...] = total[rows:].astype(high_ref.dtype)


def down(pieces, flags, w_down):
    counts = [here.shape[1] for here, _ in pieces]
    _, _, rows, _ = pieces[0][0].shape
    experts, hidden, width = w_down.shape
    tile = 2 * LANES if width % (2 * LANES) == 0 else LANES
    flat = [array for pair in pieces for array in pair]
    out = jax.ShapeDtypeStruct((rows // 2, width), jnp.bfloat16)
    return pl.pallas_call(
        functools.partial(down_kernel, counts=counts, rows=rows // 2),
        out_shape=(out, out),
        grid_spec=pltpu.PrefetchScalarGridSpec(
            num_scalar_prefetch=1,
            grid=(width // tile,),
            in_specs=[pl.BlockSpec(array.shape, lambda n, flags: (0, 0, 0, 0)) for array in flat]
            + [pl.BlockSpec(memory_space=pltpu.VMEM)],
            out_specs=[pl.BlockSpec((rows // 2, tile), lambda n, flags: (0, n))] * 2,
            scratch_shapes=[pltpu.VMEM((rows, experts * hidden), jnp.bfloat16)],
        ),
        cost_estimate=pl.CostEstimate(
            flops=2 * rows * hidden * width * experts,
            bytes_accessed=2 * hidden * width * experts,
            transcendentals=0,
        ),
        compiler_params=pltpu.CompilerParams(vmem_limit_bytes=VMEM),
        name="down",
    )(flags, *flat, w_down)


def merge_kernel(flags, keep_ref, got_ref, out_ref, kept_ref):
    quarter = out_ref.shape[3]

    def part(chip):
        span = pl.ds(pl.multiple_of(chip * quarter, quarter), quarter)
        here = keep_ref[:, :, :, span].astype(jnp.float32)
        return here + got_ref[:, :, :, span].astype(jnp.float32)

    out_ref[...] = part(1 - flags[1]).astype(out_ref.dtype)
    kept_ref[...] = part(flags[1])


def core_sum(send, keep, flags):
    got = flip(send, TENSOR, LINE, 1)
    kinds, count, rows, half = keep.shape
    shape = (kinds, count, rows, half // 2)
    spec = pl.BlockSpec((kinds, 1, rows, half), lambda e, flags: (0, e, 0, 0))
    out_spec = pl.BlockSpec((kinds, 1, rows, half // 2), lambda e, flags: (0, e, 0, 0))
    return pl.pallas_call(
        merge_kernel,
        out_shape=(
            jax.ShapeDtypeStruct(shape, jnp.bfloat16),
            jax.ShapeDtypeStruct(shape, jnp.float32),
        ),
        grid_spec=pltpu.PrefetchScalarGridSpec(
            num_scalar_prefetch=1, grid=(count,), in_specs=[spec] * 2, out_specs=(out_spec,) * 2
        ),
        cost_estimate=pl.CostEstimate(
            flops=keep.size, bytes_accessed=7 * keep.size, transcendentals=0
        ),
        compiler_params=pltpu.CompilerParams(vmem_limit_bytes=VMEM),
        name="merge",
    )(flags, keep, got)


def activate_kernel(flags, kept_ref, got_ref, *refs, first, local, active):
    gate_refs, act_ref = refs[:-1], refs[-1]
    rows = gate_refs[0].shape[0]
    which = flags[3] * local + first + pl.program_id(0)
    lane = lax.broadcasted_iota(jnp.int32, gate_refs[0].shape, 1)
    mine = (lane == which) | (lane == which + active)

    def weight(index):
        block = gate_refs[index][...]
        if len(gate_refs) > 2:
            block = jnp.where(flags[2] == 1, block, gate_refs[index + 2][...])
        return jnp.sum(jnp.where(mine, block.astype(jnp.float32), 0.0), axis=1, keepdims=True)

    for index in range(2):
        span = slice(index * rows, (index + 1) * rows)
        gate = kept_ref[0, 0, span] + got_ref[0, 0, span].astype(jnp.float32)
        up = kept_ref[1, 0, span] + got_ref[1, 0, span].astype(jnp.float32)
        act_ref[0, span] = (jax.nn.silu(gate) * up * weight(index)).astype(act_ref.dtype)


def activate(kept, got, parts, flags, first, local, depth):
    kinds, count, rows, quarter = kept.shape
    spec = pl.BlockSpec((kinds, 1, rows, quarter), lambda e, flags: (0, e, 0, 0))
    gate_spec = pl.BlockSpec((rows // 2, LANES), lambda e, flags: (0, depth // LANES))
    return pl.pallas_call(
        functools.partial(activate_kernel, first=first, local=local, active=local * LINE),
        out_shape=jax.ShapeDtypeStruct((count, rows, quarter), jnp.bfloat16),
        grid_spec=pltpu.PrefetchScalarGridSpec(
            num_scalar_prefetch=1,
            grid=(count,),
            in_specs=[spec] * 2 + [gate_spec] * len(parts),
            out_specs=pl.BlockSpec((1, rows, quarter), lambda e, flags: (e, 0, 0)),
        ),
        cost_estimate=pl.CostEstimate(
            flops=4 * kept.size, bytes_accessed=7 * kept.size, transcendentals=kept.size
        ),
        compiler_params=pltpu.CompilerParams(vmem_limit_bytes=VMEM),
        name="activate",
    )(flags, kept, got, *parts)


def spread(act, chip):
    here = jnp.stack([act, chip])
    return here, flip(here, TENSOR, 4, 1)


def layer(
    q_absorbed,
    kv_latent,
    w_values,
    w_out,
    layer_input,
    norm_gain,
    actual,
    gates,
    w_gate,
    w_up,
    w_down,
):
    local, slice_width, _ = w_gate.shape
    me, side = lax.axis_index(EXPERT), lax.axis_index(TENSOR)
    inner = (me == 1) | (me == 2)
    flags = jnp.stack([side & 1, side >> 1, inner.astype(jnp.int32), me.astype(jnp.int32)])
    inner, first_core, flags = lax.optimization_barrier((inner, (side & 1) == 0, flags))
    own = expert_rows(layer_input, norm_gain, actual, gates, slice_width, local * LINE)
    pair = lax.ppermute(own, EXPERT, OUTER)
    across = lax.ppermute(own, EXPERT, INNER)
    blocks = key_blocks(after(kv_latent, own), first_core)
    gate_near, up_near = stage(*after((w_gate, w_up), own, flags))
    pair, across, gate_near = after((pair, across, gate_near), gate_near)
    beyond = lax.ppermute(pair, EXPERT, INNER)
    out_first = lax.ppermute(across, EXPERT, OUTWARD)

    step = local // 2

    def turn(parts, index):
        send, keep = gate_up(parts, flags, gate_near, up_near, index % 2 * step, step)
        out, kept = core_sum(send, keep, flags)
        return out, kept, flip(out, TENSOR, 4, 2)

    def act(kept, got, parts, first):
        return activate(kept, got, parts, flags, first, local, slice_width)

    def spread_chip(acts):
        return flip(acts, TENSOR, 4, 2)

    out0, kept0, got0 = turn([own, pair], 0)
    out_second = lax.ppermute(beyond, EXPERT, OUTWARD)
    near_own, near_pair = after((own, pair), out0, beyond)
    out1, kept1, got1 = turn([near_own, near_pair], 1)
    near = [near_own, near_pair]
    blocks = after(blocks, out1)
    heads_out = attention(q_absorbed, blocks, w_values, flags)
    across, beyond, out_first, out_second = after(
        (across, beyond, out_first, out_second), heads_out
    )
    far = [across, beyond, out_first, out_second]
    pair_heads = lax.ppermute(heads_out, EXPERT, OUTER)
    across_heads = lax.ppermute(heads_out, EXPERT, INNER)
    out2, kept2, got2 = turn(far, 2)
    pair_heads, across_heads, far = after((pair_heads, across_heads, far), out2)
    beyond_heads = lax.ppermute(pair_heads, EXPERT, INNER)
    first_heads = lax.ppermute(across_heads, EXPERT, OUTWARD)
    out3, kept3, got3 = turn(far, 3)
    beyond_heads, got2, far = after((beyond_heads, got2, far), out3)
    second_heads = lax.ppermute(beyond_heads, EXPERT, OUTWARD)
    act2 = act(kept2, got2, far, 0)
    chip2 = spread_chip(act2)
    got0, got1 = after((got0, got1), act2)
    act0 = act(kept0, got0, near, 0)
    act1 = act(kept1, got1, near, step)
    (down_near,) = stage(after(w_down, act0, act1))
    got3 = after(got3, down_near)
    act3 = act(kept3, got3, far, step)
    chip3 = spread_chip(act3)
    act0, act1 = after((act0, act1), act3)
    chip0 = spread_chip(act0)
    chip1 = spread_chip(act1)
    first_heads, second_heads, beyond_heads = after(
        (first_heads, second_heads, beyond_heads), act3
    )
    slots = jnp.concatenate(
        [
            heads_out,
            pair_heads,
            jnp.where(inner, across_heads, first_heads),
            jnp.where(inner, beyond_heads, second_heads),
        ],
        axis=0,
    )
    partial = jnp.dot(slots, w_out, preferred_element_type=jnp.float32).astype(jnp.bfloat16)
    chip2, chip3 = after((chip2, chip3), partial)
    far_pieces = [spread(act2, chip2), spread(act3, chip3)]
    far_first, far_second = down(far_pieces, flags, down_near)
    in_second = lax.ppermute(far_second, EXPERT, INWARD)
    in_first = lax.ppermute(far_first, EXPERT, INWARD)
    partial, chip0, chip1 = after((partial, chip0, chip1), far_first)
    near_pieces = [spread(act0, chip0), spread(act1, chip1)]
    near_own, near_pair = down(near_pieces, flags, down_near)
    got_second = lax.ppermute(add(far_second, in_second), EXPERT, INNER)
    got_first = lax.ppermute(add(far_first, in_first), EXPERT, INNER)
    got_pair = lax.ppermute(add(near_pair, got_second), EXPERT, OUTER)
    mixture = (
        near_own.astype(jnp.float32) + got_first.astype(jnp.float32) + got_pair.astype(jnp.float32)
    ).astype(jnp.bfloat16)
    mine = halve(partial, TENSOR, 4, 0).astype(jnp.bfloat16)
    pairs = []
    for e in range(LINE):
        for t in range(LINE):
            slot = 2 * (t & 1) + (t >> 1)
            pairs.append((e * LINE + t, block_at(e, slot) * LINE + e))
    attended = lax.ppermute(mine, (EXPERT, TENSOR), pairs)
    return attended, mixture


def solution(mesh):
    experts, tensors = mesh.shape[EXPERT], mesh.shape[TENSOR]

    def body(
        q_absorbed,
        kv_latent,
        w_values,
        w_out,
        layer_input,
        norm_gain,
        predicted,
        actual,
        gates,
        w_gate,
        w_up,
        w_down,
    ):
        matched = jnp.any(predicted[:, None, :] == actual[:, :, None], axis=2)
        missed = jnp.sum(jnp.where(matched, 0.0, gates), axis=1)
        if experts == LINE and tensors == LINE:
            attended, mixture = layer(
                q_absorbed,
                kv_latent,
                w_values,
                w_out,
                layer_input,
                norm_gain,
                actual,
                gates,
                w_gate,
                w_up,
                w_down,
            )
            return (attended, mixture, missed)
        mixture = mix(
            layer_input, norm_gain, actual, gates, w_gate, w_up, w_down, experts, tensors
        )
        blocks = [kv_latent]
        for _ in range(1, experts):
            blocks.append(line_send(blocks[-1], EXPERT, experts, 1))
        heads_out = attend(q_absorbed, blocks, w_values)
        attended = project(heads_out, w_out, experts, tensors)
        return (attended, mixture, missed)

    placed = (
        P((GROUP, EXPERT), TENSOR),
        P((GROUP, EXPERT), None),
        P(TENSOR, None, None),
        P(TENSOR, EXPERT),
        P((GROUP, EXPERT), None),
        P(),
        P((GROUP, EXPERT), None),
        P((GROUP, EXPERT), None),
        P((GROUP, EXPERT), None),
        P(EXPERT, TENSOR, None),
        P(EXPERT, TENSOR, None),
        P(EXPERT, None, TENSOR),
    )
    return jax.shard_map(
        body,
        mesh=mesh,
        in_specs=placed,
        out_specs=(
            P((GROUP, EXPERT), TENSOR),
            P((GROUP, EXPERT), TENSOR),
            P((GROUP, EXPERT)),
        ),
        check_vma=False,
    )
```

profile of v0, /device:TPU:1, one launch (start us, length us, event | category | flops | bytes accessed | tf_op | source)
XLA Modules:
  0.0 265.7 jit_solution(5415278285331840359)
XLA Ops:
  5.8 2.2 collective-permute-start.4
  8.8 5.2 %copy-done.8 = bf16[4,1792,1024]{2,1,0:T(8,128)(2,1)S(1)} copy-done((bf16[4,1792,1024]{2,1,0:T(8,128)(2,1)S(1)}, bf16[4,1792,1024]{2,1,0:T(8,128)(2,1)}, u32[]{:S(2)}) %copy-start.8) | copy-done | bytes 14680088
  13.9 6.3 %stage.2 = (bf16[4,1792,1024]{2,1,0:T(8,128)(2,1)S(1)}, bf16[4,1792,1024]{2,1,0:T(8,128)(2,1)S(1)}) custom-call(bf16[4,1792,1024]{2,1,0:T(8,128)(2,1)S(1)} %copy-done.8, bf16[4,1792,1024]{2,1,0:T(8,128)(2,1)} %refs_1_), custom_call_target="tpu_custom_call" | custom-call | bytes 29360128 | tf_op jit(solution)/shard_map/stage/pallas_call | solution.py:360
  20.3 5.6 %gate_up.4 = (bf16[2,2,256,512]{3,2,1,0:T(8,128)(2,1)S(1)}, bf16[2,2,256,512]{3,2,1,0:T(8,128)(2,1)S(1)}) custom-call(s32[4]{0:T(128)S(1)} %pad_add_fusion.flags, bf16[128,1920]{1,0:T(8,128)(2,1)S(1)} %concatenate.15.refs_0_, bf16[128,1920]{1,0:T(8,128)(2,1)S(1)} %collective-permute-done.4.refs_1_, ...), custom_call_target="tpu_custom_call" | custom-call | flops 3758096384 | bytes 14680064 | tf_op jit(solution)/shard_map/gate_up/pallas_call | solution.py:380
  30.3 6.2 %gate_up.5 = (bf16[2,2,256,512]{3,2,1,0:T(8,128)(2,1)}, bf16[2,2,256,512]{3,2,1,0:T(8,128)(2,1)S(1)}) custom-call(s32[4]{0:T(128)S(1)} %pad_add_fusion.flags, bf16[128,1920]{1,0:T(8,128)(2,1)S(1)} %concatenate.15.refs_0_, bf16[128,1920]{1,0:T(8,128)(2,1)S(1)} %collective-permute-done.4.refs_1_, bf16[4,1792,1024]{2,1,0:T(8,128)(2,1)S(1)} %get-tuple-element.77.refs_2_.refs_4_, ...), custom_call_target="tpu_custom_call" | custom-call | flops 3758096384 | bytes 14680064 | tf_op jit(solution)/shard_map/gate_up/pallas_call | solution.py:380
  40.7 15.8 %collective-permute-start = (bf16[64,640]{1,0:T(8,128)(2,1)S(1)}, bf16[64,640]{1,0:T(8,128)(2,1)S(1)}, u32[]{:S(2)}, u32[]{:S(2)}) collective-permute-start(bf16[64,640]{1,0:T(8,128)(2,1)S(1)} %slice_select_fusion), channel_id=1, source_target_pairs={{0,4},{4,0},{8,12},{12,8},{1,5},{5,1},{9,13},{13,9},{2,6},{6,2},{1... | collective-permute-start | bytes 245768 | tf_op jit(solution)/shard_map/ppermute | solution.py:52
  59.3 2.3 collective-permute-done.1
  61.7 2.6 collective-permute-done.2
  64.3 2.2 collective-permute-start.3
  71.0 2.4 merge.5
  77.9 7.2 %attention.1 = bf16[128,2048]{1,0:T(8,128)(2,1)S(1)} custom-call(s32[4]{0:T(128)S(1)} %pad_add_fusion.flags, bf16[128,9216]{1,0:T(8,128)(2,1)S(1)} %copy-done.12, bf16[512,640]{1,0:T(8,128)(2,1)S(1)} %constant_dynamic-update-slice_fusion.even_ref, bf16[512,640]{1,0:T(8,128)(2,1)S(1)} %concatenate.18.odd_ref, bf16[16,512,128]{2,1,0:T(8,128)(2,1)S(1)} %copy-done.13), custom_call_target="tpu_custom_call" | custom-call | flops 2550136832 | bytes 2359296 | tf_op jit(solution)/shard_map/attention/pallas_call | solution.py:263
  85.1 7.9 %collective-permute-done.12.refs_3_ = bf16[128,1920]{1,0:T(8,128)(2,1)S(1)} collective-permute-done((bf16[128,1920]{1,0:T(8,128)(2,1)S(1)}, bf16[128,1920]{1,0:T(8,128)(2,1)S(1)}, u32[]{:S(2)}, u32[]{:S(2)}) %collective-permute-start.12) | collective-permute-done | bytes 491552 | tf_op jit(solution)/shard_map/ppermute | solution.py:589
  93.1 5.2 %copy-done.3 = bf16[4,1792,1024]{2,1,0:T(8,128)(2,1)S(1)} copy-done((bf16[4,1792,1024]{2,1,0:T(8,128)(2,1)S(1)}, bf16[4,1792,1024]{2,1,0:T(8,128)(2,1)}, u32[]{:S(2)}) %copy-start.3) | copy-done | bytes 14680088
  98.3 5.6 %gate_up.6 = (bf16[2,2,256,512]{3,2,1,0:T(8,128)(2,1)S(1)}, bf16[2,2,256,512]{3,2,1,0:T(8,128)(2,1)S(1)}) custom-call(s32[4]{0:T(128)S(1)} %pad_add_fusion.flags, bf16[128,1920]{1,0:T(8,128)(2,1)S(1)} %collective-permute-done.5.refs_0_, bf16[128,1920]{1,0:T(8,128)(2,1)S(1)} %collective-permute-done.7.refs_1_, ...), custom_call_target="tpu_custom_call" | custom-call | flops 3758096384 | bytes 14680064 | tf_op jit(solution)/shard_map/gate_up/pallas_call | solution.py:380
  108.6 11.0 %collective-permute-done.9 = bf16[128,2048]{1,0:T(8,128)(2,1)S(1)} collective-permute-done((bf16[128,2048]{1,0:T(8,128)(2,1)S(1)}, bf16[128,2048]{1,0:T(8,128)(2,1)S(1)}, u32[]{:S(2)}, u32[]{:S(2)}) %collective-permute-start.9) | collective-permute-done | bytes 524320 | tf_op jit(solution)/shard_map/ppermute | solution.py:599
  119.6 5.6 %gate_up.7 = (bf16[2,2,256,512]{3,2,1,0:T(8,128)(2,1)S(1)}, bf16[2,2,256,512]{3,2,1,0:T(8,128)(2,1)S(1)}) custom-call(s32[4]{0:T(128)S(1)} %pad_add_fusion.flags, bf16[128,1920]{1,0:T(8,128)(2,1)S(1)} %collective-permute-done.5.refs_0_, bf16[128,1920]{1,0:T(8,128)(2,1)S(1)} %collective-permute-done.7.refs_1_, ...), custom_call_target="tpu_custom_call" | custom-call | flops 3758096384 | bytes 14680064 | tf_op jit(solution)/shard_map/gate_up/pallas_call | solution.py:380
  132.3 8.1 %collective-permute-done.16.got_ref = bf16[2,2,256,256]{3,2,1,0:T(8,128)(2,1)S(1)} collective-permute-done((bf16[2,2,256,256]{3,2,1,0:T(8,128)(2,1)S(1)}, bf16[2,2,256,256]{3,2,1,0:T(8,128)(2,1)S(1)}, u32[]{:S(2)}, u32[]{:S(2)}) %collective-permute-start.16) | collective-permute-done | bytes 524320 | tf_op jit(solution)/shard_map/ppermute | solution.py:52
  142.7 8.9 %collective-permute-done.20.got_ref = bf16[2,2,256,256]{3,2,1,0:T(8,128)(2,1)S(1)} collective-permute-done((bf16[2,2,256,256]{3,2,1,0:T(8,128)(2,1)S(1)}, bf16[2,2,256,256]{3,2,1,0:T(8,128)(2,1)S(1)}, u32[]{:S(2)}, u32[]{:S(2)}) %collective-permute-start.20) | collective-permute-done | bytes 524320 | tf_op jit(solution)/shard_map/ppermute | solution.py:52
  152.8 10.1 %collective-permute-done.21.got_ref = bf16[2,2,256,256]{3,2,1,0:T(8,128)(2,1)S(1)} collective-permute-done((bf16[2,2,256,256]{3,2,1,0:T(8,128)(2,1)S(1)}, bf16[2,2,256,256]{3,2,1,0:T(8,128)(2,1)S(1)}, u32[]{:S(2)}, u32[]{:S(2)}) %collective-permute-start.21) | collective-permute-done | bytes 524320 | tf_op jit(solution)/shard_map/ppermute | solution.py:52
  164.8 5.2 %copy-done.9 = bf16[4,1024,1792]{2,1,0:T(8,128)(2,1)S(1)} copy-done((bf16[4,1024,1792]{2,1,0:T(8,128)(2,1)S(1)}, bf16[4,1024,1792]{2,1,0:T(8,128)(2,1)}, u32[]{:S(2)}) %copy-start.9) | copy-done | bytes 14680088
  171.0 5.2 %copy-done.5 = bf16[4,1024,1792]{2,1,0:T(8,128)(2,1)} copy-done((bf16[4,1024,1792]{2,1,0:T(8,128)(2,1)}, bf16[4,1024,1792]{2,1,0:T(8,128)(2,1)S(1)}, u32[]{:S(2)}) %copy-start.5) | copy-done | bytes 14680088
  178.6 6.6 %convolution_convert_fusion = bf16[512,1792]{1,0:T(8,128)(2,1)} fusion(bf16[2048,1792]{1,0:T(8,128)(2,1)S(1)} %bitcast.39, bf16[128,2048]{1,0:T(8,128)(2,1)S(1)} %get-tuple-element.142, bf16[128,2048]{1,0:T(8,128)(2,1)S(1)} %get-tuple-element.143, bf16[128,2048]{1,0:T(8,128)(2,1)S(1)} %collective-permute-done.9, bf16[128,2048]{1,0:T(8,128)(2,1)S(1)} %attention.1), kind=kOutput, calls=%fused_computation.1 | convolution fusion | flops 3767402496 | bytes 11272192 | tf_op jit(solution)/shard_map/dot_general | solution.py:632
  189.2 5.2 %copy-done.6 = bf16[4,1024,1792]{2,1,0:T(8,128)(2,1)S(1)} copy-done((bf16[4,1024,1792]{2,1,0:T(8,128)(2,1)S(1)}, bf16[4,1024,1792]{2,1,0:T(8,128)(2,1)}, u32[]{:S(2)}) %copy-start.6) | copy-done | bytes 14680088
  194.4 6.2 %down.2 = (bf16[128,1792]{1,0:T(8,128)(2,1)S(1)}, bf16[128,1792]{1,0:T(8,128)(2,1)S(1)}) custom-call(s32[4]{0:T(128)S(1)} %pad_add_fusion.flags, bf16[2,2,256,256]{3,2,1,0:T(8,128)(2,1)S(1)} %pad_maximum_fusion.refs_0_, bf16[2,2,256,256]{3,2,1,0:T(8,128)(2,1)S(1)} %collective-permute-done.26.refs_1_, bf16[2,2,256,256]{3,2,1,0:T(8,128)(2,1)S(1)} %pad_maximum_fusion.1.refs_2_, ...), custom_call_target="tpu_custom_call" | custom-call | flops 3758096384 | bytes 14680064 | tf_op jit(solution)/shard_map/down/pallas_call | solution.py:446
  200.6 5.4 %collective-permute-start.33 = (bf16[128,1792]{1,0:T(8,128)(2,1)S(1)}, bf16[128,1792]{1,0:T(8,128)(2,1)S(1)}, u32[]{:S(2)}, u32[]{:S(2)}) collective-permute-start(bf16[128,1792]{1,0:T(8,128)(2,1)S(1)} %get-tuple-element.130), channel_id=1, source_target_pairs={{0,4},{12,8},{1,5},{13,9},{2,6},{14,10},{3,7},{15,11},{16,20},{28,... | collective-permute-start | bytes 1376264 | tf_op jit(solution)/shard_map/ppermute | solution.py:637
  209.5 5.4 %collective-permute-done.33 = bf16[128,1792]{1,0:T(8,128)(2,1)S(1)} collective-permute-done((bf16[128,1792]{1,0:T(8,128)(2,1)S(1)}, bf16[128,1792]{1,0:T(8,128)(2,1)S(1)}, u32[]{:S(2)}, u32[]{:S(2)}) %collective-permute-start.33) | collective-permute-done | bytes 458784 | tf_op jit(solution)/shard_map/ppermute | solution.py:637
  215.7 9.0 %collective-permute-done.35 = bf16[128,1792]{1,0:T(8,128)(2,1)S(1)} collective-permute-done((bf16[128,1792]{1,0:T(8,128)(2,1)S(1)}, bf16[128,1792]{1,0:T(8,128)(2,1)S(1)}, u32[]{:S(2)}, u32[]{:S(2)}) %collective-permute-start.35) | collective-permute-done | bytes 458784 | tf_op jit(solution)/shard_map/ppermute | solution.py:636
  225.6 6.2 %down.3 = (bf16[128,1792]{1,0:T(8,128)(2,1)S(1)}, bf16[128,1792]{1,0:T(8,128)(2,1)S(1)}) custom-call(s32[4]{0:T(128)S(1)} %pad_add_fusion.flags, bf16[2,2,256,256]{3,2,1,0:T(8,128)(2,1)S(1)} %pad_maximum_fusion.2.refs_0_, bf16[2,2,256,256]{3,2,1,0:T(8,128)(2,1)S(1)} %collective-permute-done.31.refs_1_, ...), custom_call_target="tpu_custom_call" | custom-call | flops 3758096384 | bytes 14680064 | tf_op jit(solution)/shard_map/down/pallas_call | solution.py:446
  232.7 6.7 %collective-permute-start.37 = (bf16[128,1792]{1,0:T(8,128)(2,1)S(1)}, bf16[128,1792]{1,0:T(8,128)(2,1)S(1)}, u32[]{:S(2)}, u32[]{:S(2)}) collective-permute-start(bf16[128,1792]{1,0:T(8,128)(2,1)S(1)} %add_convert_fusion.2), channel_id=1, source_target_pairs={{0,4},{4,0},{8,12},{12,8},{1,5},{5,1},{9,13},{13,9},{2,6},{6,2},{1... | collective-permute-start | bytes 1376264 | tf_op jit(solution)/shard_map/ppermute | solution.py:643
  239.4 3.2 %collective-permute-done.29 = bf16[128,1792]{1,0:T(8,128)(2,1)S(1)} collective-permute-done((bf16[128,1792]{1,0:T(8,128)(2,1)S(1)}, bf16[128,1792]{1,0:T(8,128)(2,1)S(1)}, u32[]{:S(2)}, u32[]{:S(2)}) %collective-permute-start.29) | collective-permute-done | bytes 458784 | tf_op jit(solution)/shard_map/ppermute | solution.py:52
  242.7 9.1 %collective-permute-start.30 = (bf16[128,1792]{1,0:T(8,128)(2,1)S(1)}, bf16[128,1792]{1,0:T(8,128)(2,1)S(1)}, u32[]{:S(2)}, u32[]{:S(2)}) collective-permute-start(bf16[128,1792]{1,0:T(8,128)(2,1)S(1)} %add_convert_fusion.5), channel_id=1, source_target_pairs={{0,0},{1,8},{2,4},{3,12},{4,5},{5,9},{6,1},{7,13},{8,10},{9,6},{10... | collective-permute-start | bytes 1376264 | tf_op jit(solution)/shard_map/ppermute | solution.py:653
  252.8 12.2 %collective-permute-done.30 = bf16[128,1792]{1,0:T(8,128)(2,1)S(1)} collective-permute-done((bf16[128,1792]{1,0:T(8,128)(2,1)S(1)}, bf16[128,1792]{1,0:T(8,128)(2,1)S(1)}, u32[]{:S(2)}, u32[]{:S(2)}) %collective-permute-start.30) | collective-permute-done | bytes 458784 | tf_op jit(solution)/shard_map/ppermute | solution.py:653
  (147 shorter events, 58.6 us)
Async XLA Ops:
  5.8 14.5 %collective-permute-start.4 = (bf16[128,1920]{1,0:T(8,128)(2,1)S(1)}, bf16[128,1920]{1,0:T(8,128)(2,1)S(1)}, u32[]{:S(2)}, u32[]{:S(2)}) collective-permute-start(bf16[128,1920]{1,0:T(8,128)(2,1)S(1)} %concatenate.15.refs_0_), channel_id=1, source_target_pairs={{0,4},{4,0},{8,12},{12,8},{1,5},{5,1},{9,13},{13,9},{2,6},{6,2},{1... | collective-permute-start | bytes 1474568 | tf_op jit(solution)/shard_map/ppermute | solution.py:567
  8.0 12.3 %collective-permute-start.5 = (bf16[128,1920]{1,0:T(8,128)(2,1)S(1)}, bf16[128,1920]{1,0:T(8,128)(2,1)S(1)}, u32[]{:S(2)}, u32[]{:S(2)}) collective-permute-start(bf16[128,1920]{1,0:T(8,128)(2,1)S(1)} %concatenate.15.refs_0_), channel_id=1, source_target_pairs={{4,8},{8,4},{5,9},{9,5},{6,10},{10,6},{7,11},{11,7},{20,24},{24,20... | collective-permute-start | bytes 1474568 | tf_op jit(solution)/shard_map/ppermute | solution.py:568
  37.5 33.5 %collective-permute-start.8 = (bf16[2,2,256,512]{3,2,1,0:T(8,128)(2,1)}, bf16[2,2,256,512]{3,2,1,0:T(8,128)(2,1)}, u32[]{:S(2)}, u32[]{:S(2)}) collective-permute-start(bf16[2,2,256,512]{3,2,1,0:T(8,128)(2,1)} %get-tuple-element.85), channel_id=1, source_target_pairs={{0,1},{1,0},{2,3},{3,2},{4,5},{5,4},{6,7},{7,6},{8,9},{9,8},{10,11... | collective-permute-start | bytes 3145736 | tf_op jit(solution)/shard_map/ppermute | solution.py:52
  40.7 18.6 %collective-permute-start = (bf16[64,640]{1,0:T(8,128)(2,1)S(1)}, bf16[64,640]{1,0:T(8,128)(2,1)S(1)}, u32[]{:S(2)}, u32[]{:S(2)}) collective-permute-start(bf16[64,640]{1,0:T(8,128)(2,1)S(1)} %slice_select_fusion), channel_id=1, source_target_pairs={{0,4},{4,0},{8,12},{12,8},{1,5},{5,1},{9,13},{13,9},{2,6},{6,2},{1... | collective-permute-start | bytes 245768 | tf_op jit(solution)/shard_map/ppermute | solution.py:52
  56.5 5.1 %collective-permute-start.1 = (bf16[64,640]{1,0:T(8,128)(2,1)S(1)}, bf16[64,640]{1,0:T(8,128)(2,1)S(1)}, u32[]{:S(2)}, u32[]{:S(2)}) collective-permute-start(bf16[64,640]{1,0:T(8,128)(2,1)S(1)} %slice_select_fusion), channel_id=1, source_target_pairs={{0,8},{4,12},{8,0},{12,4},{1,9},{5,13},{9,1},{13,5},{2,10},{6,14},... | collective-permute-start | bytes 245768 | tf_op jit(solution)/shard_map/ppermute | solution.py:52
  57.1 7.2 %collective-permute-start.2 = (bf16[64,640]{1,0:T(8,128)(2,1)S(1)}, bf16[64,640]{1,0:T(8,128)(2,1)S(1)}, u32[]{:S(2)}, u32[]{:S(2)}) collective-permute-start(bf16[64,640]{1,0:T(8,128)(2,1)S(1)} %slice_select_fusion), channel_id=1, source_target_pairs={{0,12},{4,8},{8,4},{12,0},{1,13},{5,9},{9,5},{13,1},{2,14},{6,10},... | collective-permute-start | bytes 245768 | tf_op jit(solution)/shard_map/ppermute | solution.py:52
  67.8 17.3 %collective-permute-start.11 = (bf16[128,1920]{1,0:T(8,128)(2,1)S(1)}, bf16[128,1920]{1,0:T(8,128)(2,1)S(1)}, u32[]{:S(2)}, u32[]{:S(2)}) collective-permute-start(bf16[128,1920]{1,0:T(8,128)(2,1)S(1)} %collective-permute-done.5.refs_0_), channel_id=1, source_target_pairs={{4,0},{8,12},{5,1},{9,13},{6,2},{10,14},{7,3},{11,15},{20,16},{24,... | collective-permute-start | bytes 1474568 | tf_op jit(solution)/shard_map/ppermute | solution.py:573
  69.4 23.7 %collective-permute-start.12 = (bf16[128,1920]{1,0:T(8,128)(2,1)S(1)}, bf16[128,1920]{1,0:T(8,128)(2,1)S(1)}, u32[]{:S(2)}, u32[]{:S(2)}) collective-permute-start(bf16[128,1920]{1,0:T(8,128)(2,1)S(1)} %collective-permute-done.7.refs_1_), channel_id=1, source_target_pairs={{4,0},{8,12},{5,1},{9,13},{6,2},{10,14},{7,3},{11,15},{20,16},{24,... | collective-permute-start | bytes 1474568 | tf_op jit(solution)/shard_map/ppermute | solution.py:589
  106.1 13.5 %collective-permute-start.9 = (bf16[128,2048]{1,0:T(8,128)(2,1)S(1)}, bf16[128,2048]{1,0:T(8,128)(2,1)S(1)}, u32[]{:S(2)}, u32[]{:S(2)}) collective-permute-start(bf16[128,2048]{1,0:T(8,128)(2,1)S(1)} %attention.1), channel_id=1, source_target_pairs={{0,4},{4,0},{8,12},{12,8},{1,5},{5,1},{9,13},{13,9},{2,6},{6,2},{1... | collective-permute-start | bytes 1572872 | tf_op jit(solution)/shard_map/ppermute | solution.py:599
  125.2 4.3 %collective-permute-start.17 = (bf16[2,2,256,512]{3,2,1,0:T(8,128)(2,1)S(1)}, bf16[2,2,256,512]{3,2,1,0:T(8,128)(2,1)S(1)}, u32[]{:S(2)}, u32[]{:S(2)}) collective-permute-start(bf16[2,2,256,512]{3,2,1,0:T(8,128)(2,1)S(1)} %get-tuple-element.107), channel_id=1, source_target_pairs={{0,1},{1,0},{2,3},{3,2},{4,5},{5,4},{6,7},{7,6},{8,9},{9,8},{10,11... | collective-permute-start | bytes 3145736 | tf_op jit(solution)/shard_map/ppermute | solution.py:52
  126.2 4.8 %collective-permute-start.15 = (bf16[128,2048]{1,0:T(8,128)(2,1)S(1)}, bf16[128,2048]{1,0:T(8,128)(2,1)S(1)}, u32[]{:S(2)}, u32[]{:S(2)}) collective-permute-start(bf16[128,2048]{1,0:T(8,128)(2,1)S(1)} %collective-permute-done.9), channel_id=1, source_target_pairs={{4,8},{8,4},{5,9},{9,5},{6,10},{10,6},{7,11},{11,7},{20,24},{24,20... | collective-permute-start | bytes 1572872 | tf_op jit(solution)/shard_map/ppermute | solution.py:603
  126.9 13.5 %collective-permute-start.16 = (bf16[2,2,256,256]{3,2,1,0:T(8,128)(2,1)S(1)}, bf16[2,2,256,256]{3,2,1,0:T(8,128)(2,1)S(1)}, u32[]{:S(2)}, u32[]{:S(2)}) collective-permute-start(bf16[2,2,256,256]{3,2,1,0:T(8,128)(2,1)S(1)} %get-tuple-element.98), channel_id=1, source_target_pairs={{0,2},{1,3},{2,0},{3,1},{4,6},{5,7},{6,4},{7,5},{8,10},{9,11},{10,... | collective-permute-start | bytes 1572872 | tf_op jit(solution)/shard_map/ppermute | solution.py:52
  128.1 23.5 %collective-permute-start.20 = (bf16[2,2,256,256]{3,2,1,0:T(8,128)(2,1)S(1)}, bf16[2,2,256,256]{3,2,1,0:T(8,128)(2,1)S(1)}, u32[]{:S(2)}, u32[]{:S(2)}) collective-permute-start(bf16[2,2,256,256]{3,2,1,0:T(8,128)(2,1)S(1)} %get-tuple-element.81), channel_id=1, source_target_pairs={{0,2},{1,3},{2,0},{3,1},{4,6},{5,7},{6,4},{7,5},{8,10},{9,11},{10,... | collective-permute-start | bytes 1572872 | tf_op jit(solution)/shard_map/ppermute | solution.py:52
  128.4 34.5 %collective-permute-start.21 = (bf16[2,2,256,256]{3,2,1,0:T(8,128)(2,1)S(1)}, bf16[2,2,256,256]{3,2,1,0:T(8,128)(2,1)S(1)}, u32[]{:S(2)}, u32[]{:S(2)}) collective-permute-start(bf16[2,2,256,256]{3,2,1,0:T(8,128)(2,1)S(1)} %copy-done.15), channel_id=1, source_target_pairs={{0,2},{1,3},{2,0},{3,1},{4,6},{5,7},{6,4},{7,5},{8,10},{9,11},{10,... | collective-permute-start | bytes 1572872 | tf_op jit(solution)/shard_map/ppermute | solution.py:52
  130.7 45.5 %collective-permute-start.19 = (bf16[2,2,256,256]{3,2,1,0:T(8,128)(2,1)S(1)}, bf16[2,2,256,256]{3,2,1,0:T(8,128)(2,1)S(1)}, u32[]{:S(2)}, u32[]{:S(2)}) collective-permute-start(bf16[2,2,256,256]{3,2,1,0:T(8,128)(2,1)S(1)} %get-tuple-element.108), channel_id=1, source_target_pairs={{0,2},{1,3},{2,0},{3,1},{4,6},{5,7},{6,4},{7,5},{8,10},{9,11},{10,... | collective-permute-start | bytes 1572872 | tf_op jit(solution)/shard_map/ppermute | solution.py:52
  131.0 47.4 %collective-permute-start.14 = (bf16[128,2048]{1,0:T(8,128)(2,1)S(1)}, bf16[128,2048]{1,0:T(8,128)(2,1)S(1)}, u32[]{:S(2)}, u32[]{:S(2)}) collective-permute-start(bf16[128,2048]{1,0:T(8,128)(2,1)S(1)} %collective-permute-done.10), channel_id=1, source_target_pairs={{4,0},{8,12},{5,1},{9,13},{6,2},{10,14},{7,3},{11,15},{20,16},{24,... | collective-permute-start | bytes 1572872 | tf_op jit(solution)/shard_map/ppermute | solution.py:604
  140.4 38.1 %collective-permute-start.18 = (bf16[128,2048]{1,0:T(8,128)(2,1)S(1)}, bf16[128,2048]{1,0:T(8,128)(2,1)S(1)}, u32[]{:S(2)}, u32[]{:S(2)}) collective-permute-start(bf16[128,2048]{1,0:T(8,128)(2,1)S(1)} %collective-permute-done.15), channel_id=1, source_target_pairs={{4,0},{8,12},{5,1},{9,13},{6,2},{10,14},{7,3},{11,15},{20,16},{24,... | collective-permute-start | bytes 1572872 | tf_op jit(solution)/shard_map/ppermute | solution.py:607
  151.6 33.5 %collective-permute-start.24 = (bf16[2,256,256]{2,1,0:T(8,128)(2,1)S(1)}, bf16[2,256,256]{2,1,0:T(8,128)(2,1)S(1)}, u32[]{:S(2)}, u32[]{:S(2)}) collective-permute-start(bf16[2,256,256]{2,1,0:T(8,128)(2,1)S(1)} %activate.4), channel_id=1, source_target_pairs={{0,2},{1,3},{2,0},{3,1},{4,6},{5,7},{6,4},{7,5},{8,10},{9,11},{10,... | collective-permute-start | bytes 786440 | tf_op jit(solution)/shard_map/ppermute | solution.py:52
  177.2 8.0 %collective-permute-start.25 = (bf16[2,256,256]{2,1,0:T(8,128)(2,1)S(1)}, bf16[2,256,256]{2,1,0:T(8,128)(2,1)S(1)}, u32[]{:S(2)}, u32[]{:S(2)}) collective-permute-start(bf16[2,256,256]{2,1,0:T(8,128)(2,1)S(1)} %activate.7), channel_id=1, source_target_pairs={{0,2},{1,3},{2,0},{3,1},{4,6},{5,7},{6,4},{7,5},{8,10},{9,11},{10,... | collective-permute-start | bytes 786440 | tf_op jit(solution)/shard_map/ppermute | solution.py:52
  185.2 3.9 %collective-permute-start.27 = (bf16[2,2,256,256]{3,2,1,0:T(8,128)(2,1)S(1)}, bf16[2,2,256,256]{3,2,1,0:T(8,128)(2,1)S(1)}, u32[]{:S(2)}, u32[]{:S(2)}) collective-permute-start(bf16[2,2,256,256]{3,2,1,0:T(8,128)(2,1)S(1)} %pad_maximum_fusion.1.refs_2_), channel_id=1, source_target_pairs={{0,1},{1,0},{2,3},{3,2},{4,5},{5,4},{6,7},{7,6},{8,9},{9,8},{10,11... | collective-permute-start | bytes 1572872 | tf_op jit(solution)/shard_map/ppermute | solution.py:52
  187.7 18.3 %collective-permute-start.22 = (bf16[2,256,256]{2,1,0:T(8,128)(2,1)S(1)}, bf16[2,256,256]{2,1,0:T(8,128)(2,1)S(1)}, u32[]{:S(2)}, u32[]{:S(2)}) collective-permute-start(bf16[2,256,256]{2,1,0:T(8,128)(2,1)S(1)} %activate.5), channel_id=1, source_target_pairs={{0,2},{1,3},{2,0},{3,1},{4,6},{5,7},{6,4},{7,5},{8,10},{9,11},{10,... | collective-permute-start | bytes 786440 | tf_op jit(solution)/shard_map/ppermute | solution.py:52
  188.2 17.8 %collective-permute-start.23 = (bf16[2,256,256]{2,1,0:T(8,128)(2,1)S(1)}, bf16[2,256,256]{2,1,0:T(8,128)(2,1)S(1)}, u32[]{:S(2)}, u32[]{:S(2)}) collective-permute-start(bf16[2,256,256]{2,1,0:T(8,128)(2,1)S(1)} %activate.6), channel_id=1, source_target_pairs={{0,2},{1,3},{2,0},{3,1},{4,6},{5,7},{6,4},{7,5},{8,10},{9,11},{10,... | collective-permute-start | bytes 786440 | tf_op jit(solution)/shard_map/ppermute | solution.py:52
  200.6 14.3 %collective-permute-start.33 = (bf16[128,1792]{1,0:T(8,128)(2,1)S(1)}, bf16[128,1792]{1,0:T(8,128)(2,1)S(1)}, u32[]{:S(2)}, u32[]{:S(2)}) collective-permute-start(bf16[128,1792]{1,0:T(8,128)(2,1)S(1)} %get-tuple-element.130), channel_id=1, source_target_pairs={{0,4},{12,8},{1,5},{13,9},{2,6},{14,10},{3,7},{15,11},{16,20},{28,... | collective-permute-start | bytes 1376264 | tf_op jit(solution)/shard_map/ppermute | solution.py:637
  206.1 19.5 %collective-permute-start.32 = (bf16[2,2,256,256]{3,2,1,0:T(8,128)(2,1)S(1)}, bf16[2,2,256,256]{3,2,1,0:T(8,128)(2,1)S(1)}, u32[]{:S(2)}, u32[]{:S(2)}) collective-permute-start(bf16[2,2,256,256]{3,2,1,0:T(8,128)(2,1)S(1)} %pad_maximum_fusion.3.refs_2_), channel_id=1, source_target_pairs={{0,1},{1,0},{2,3},{3,2},{4,5},{5,4},{6,7},{7,6},{8,9},{9,8},{10,11... | collective-permute-start | bytes 1572872 | tf_op jit(solution)/shard_map/ppermute | solution.py:52
  207.5 18.1 %collective-permute-start.31 = (bf16[2,2,256,256]{3,2,1,0:T(8,128)(2,1)S(1)}, bf16[2,2,256,256]{3,2,1,0:T(8,128)(2,1)S(1)}, u32[]{:S(2)}, u32[]{:S(2)}) collective-permute-start(bf16[2,2,256,256]{3,2,1,0:T(8,128)(2,1)S(1)} %pad_maximum_fusion.2.refs_0_), channel_id=1, source_target_pairs={{0,1},{1,0},{2,3},{3,2},{4,5},{5,4},{6,7},{7,6},{8,9},{9,8},{10,11... | collective-permute-start | bytes 1572872 | tf_op jit(solution)/shard_map/ppermute | solution.py:52
  207.5 17.2 %collective-permute-start.35 = (bf16[128,1792]{1,0:T(8,128)(2,1)S(1)}, bf16[128,1792]{1,0:T(8,128)(2,1)S(1)}, u32[]{:S(2)}, u32[]{:S(2)}) collective-permute-start(bf16[128,1792]{1,0:T(8,128)(2,1)S(1)} %get-tuple-element.136), channel_id=1, source_target_pairs={{0,4},{12,8},{1,5},{13,9},{2,6},{14,10},{3,7},{15,11},{16,20},{28,... | collective-permute-start | bytes 1376264 | tf_op jit(solution)/shard_map/ppermute | solution.py:636
  209.0 22.8 %collective-permute-start.28 = (bf16[256,1792]{1,0:T(8,128)(2,1)S(1)}, bf16[256,1792]{1,0:T(8,128)(2,1)S(1)}, u32[]{:S(2)}, u32[]{:S(2)}) collective-permute-start(bf16[256,1792]{1,0:T(8,128)(2,1)S(1)} %broadcast_select_fusion), channel_id=1, source_target_pairs={{0,1},{1,0},{2,3},{3,2},{4,5},{5,4},{6,7},{7,6},{8,9},{9,8},{10,11... | collective-permute-start | bytes 2752520 | tf_op jit(solution)/shard_map/ppermute | solution.py:52
  215.0 36.8 %collective-permute-start.34 = (bf16[128,1792]{1,0:T(8,128)(2,1)S(1)}, bf16[128,1792]{1,0:T(8,128)(2,1)S(1)}, u32[]{:S(2)}, u32[]{:S(2)}) collective-permute-start(bf16[128,1792]{1,0:T(8,128)(2,1)S(1)} %add_convert_fusion.4), channel_id=1, source_target_pairs={{4,8},{8,4},{5,9},{9,5},{6,10},{10,6},{7,11},{11,7},{20,24},{24,20... | collective-permute-start | bytes 1376264 | tf_op jit(solution)/shard_map/ppermute | solution.py:642
  224.9 7.7 %collective-permute-start.36 = (bf16[128,1792]{1,0:T(8,128)(2,1)S(1)}, bf16[128,1792]{1,0:T(8,128)(2,1)S(1)}, u32[]{:S(2)}, u32[]{:S(2)}) collective-permute-start(bf16[128,1792]{1,0:T(8,128)(2,1)S(1)} %add_convert_fusion.3), channel_id=1, source_target_pairs={{4,8},{8,4},{5,9},{9,5},{6,10},{10,6},{7,11},{11,7},{20,24},{24,20... | collective-permute-start | bytes 1376264 | tf_op jit(solution)/shard_map/ppermute | solution.py:641
  232.2 10.3 %collective-permute-start.29 = (bf16[128,1792]{1,0:T(8,128)(2,1)S(1)}, bf16[128,1792]{1,0:T(8,128)(2,1)S(1)}, u32[]{:S(2)}, u32[]{:S(2)}) collective-permute-start(bf16[128,1792]{1,0:T(8,128)(2,1)S(1)} %broadcast_select_fusion.3), channel_id=1, source_target_pairs={{0,2},{1,3},{2,0},{3,1},{4,6},{5,7},{6,4},{7,5},{8,10},{9,11},{10,... | collective-permute-start | bytes 1376264 | tf_op jit(solution)/shard_map/ppermute | solution.py:52
  232.7 19.1 %collective-permute-start.37 = (bf16[128,1792]{1,0:T(8,128)(2,1)S(1)}, bf16[128,1792]{1,0:T(8,128)(2,1)S(1)}, u32[]{:S(2)}, u32[]{:S(2)}) collective-permute-start(bf16[128,1792]{1,0:T(8,128)(2,1)S(1)} %add_convert_fusion.2), channel_id=1, source_target_pairs={{0,4},{4,0},{8,12},{12,8},{1,5},{5,1},{9,13},{13,9},{2,6},{6,2},{1... | collective-permute-start | bytes 1376264 | tf_op jit(solution)/shard_map/ppermute | solution.py:643
  242.7 22.2 %collective-permute-start.30 = (bf16[128,1792]{1,0:T(8,128)(2,1)S(1)}, bf16[128,1792]{1,0:T(8,128)(2,1)S(1)}, u32[]{:S(2)}, u32[]{:S(2)}) collective-permute-start(bf16[128,1792]{1,0:T(8,128)(2,1)S(1)} %add_convert_fusion.5), channel_id=1, source_target_pairs={{0,0},{1,8},{2,4},{3,12},{4,5},{5,9},{6,1},{7,13},{8,10},{9,6},{10... | collective-permute-start | bytes 1376264 | tf_op jit(solution)/shard_map/ppermute | solution.py:653
  (28 other events, 273.5 us)
where the time goes:
time: 267 us; the launch traced here: 266 us
  waiting for transfers between devices  83.5 us (31%)
  starting transfers between devices  70.8 us (27%)
  Pallas kernels  59.5 us (22%)
  local copies, waits for them, and re-layouts  36.1 us (14%)
  other arithmetic  7.95 us (3%)
  matrix products  6.55 us (2%)
    ppermute x22, waiting for transfers between devices, flip(): return lax.ppermute(value, axis, [(i, i ^ bit) for i in range(size)])  37.9 us
    ppermute x22, starting transfers between devices, flip(): return lax.ppermute(value, axis, [(i, i ^ bit) for i in range(size)])  35 us
    unnamed x48, local copies, waits for them, and re-layouts  31.8 us
    pallas_call x4, Pallas kernels, gate_up(): pl.pallas_call(functools.partial(rows_kernel, parts=len(parts), rows=rows...  23.1 us
    pallas_call x2, Pallas kernels, down(): pl.pallas_call(functools.partial(down_kernel, counts=counts, rows=rows //...  12.4 us
    ppermute x1, waiting for transfers between devices, layer(): attended = lax.ppermute(mine, (EXPERT, TENSOR), pairs)  12.2 us
    ppermute x1, waiting for transfers between devices, layer(): pair_heads = lax.ppermute(heads_out, EXPERT, OUTER)  11 us
    ppermute x1, starting transfers between devices, layer(): attended = lax.ppermute(mine, (EXPERT, TENSOR), pairs)  9.06 us
  transfers between devices with their start and end apart: 38, of which 16 were waited for; matrix products, arithmetic and copies ran while one was open for 5% of the time, Pallas kernels for 14%

commit v1 on v0

--- a/solution.py
+++ b/solution.py
@@ -190,6 +190,7 @@
 
 LINE = 4
 VMEM = 10 * 1024 * 1024
+STAGE_VMEM = 30 * 1024 * 1024
 OUTER = [(0, 1), (1, 0), (2, 3), (3, 2)]
 INNER = [(1, 2), (2, 1)]
 OUTWARD = [(1, 0), (2, 3)]
@@ -285,15 +286,17 @@
     )(flags, q_absorbed, keys, odd, w_values)
 
 
-def key_blocks(kv_latent, first_core):
+def key_halves(kv_latent, first_core):
     rows, width = kv_latent.shape
     half = rows // 2
     whole = jnp.pad(kv_latent, ((0, 0), (0, -width % LANES)))
     mine = jnp.where(first_core, whole[:half], whole[half:])
-    got = []
-    for step in range(1, LINE):
-        got.append(flip(mine, EXPERT, LINE, step))
-    got = jnp.stack(got)
+    pair = flip(mine, EXPERT, LINE, 1)
+    others = flip(jnp.stack([mine, pair]), EXPERT, LINE, 2)
+    return whole, jnp.concatenate([pair[None], others])
+
+
+def key_blocks(whole, got, first_core):
     other = flip(got, TENSOR, LINE, 1)
     full = jnp.concatenate(
         [jnp.where(first_core, got, other), jnp.where(first_core, other, got)], axis=1
@@ -301,11 +304,11 @@
     return [whole] + [full[index] for index in range(LINE - 1)]
 
 
-def rows_kernel(flags, *refs, parts, rows, first):
-    part_refs, (gate_ref, up_ref, send_ref, keep_ref, tokens) = refs[:parts], refs[parts:]
-    item, side = pl.program_id(0), pl.program_id(1)
-
-    @pl.when((item == 0) & (side == 0))
+def rows_kernel(flags, *refs, parts, rows, side):
+    part_refs, (gate_ref, up_ref, out_ref, tokens) = refs[:parts], refs[parts:]
+    item = pl.program_id(0)
+
+    @pl.when(item == 0)
     def _():
         if parts == 2:
             tokens[:rows] = part_refs[0][...]
@@ -322,75 +325,64 @@
                 tokens[:rows] = part_refs[2][...]
                 tokens[rows:] = part_refs[3][...]
 
-    def both(out_ref, core):
-        half = gate_ref.shape[2] // 2
-        span = pl.ds(pl.multiple_of(core * half, half), half)
-        for index, weight_ref in enumerate((gate_ref, up_ref)):
-            out_ref[index, 0] = jnp.dot(
-                tokens[...], weight_ref[first + item, :, span], preferred_element_type=jnp.float32
-            ).astype(out_ref.dtype)
-
-    @pl.when(side == 0)
-    def _():
-        both(send_ref, 1 - flags[0])
-
-    @pl.when(side == 1)
-    def _():
-        both(keep_ref, flags[0])
-
-
-def stage_kernel(*refs):
+    half = gate_ref.shape[2] // 2
+    core = flags[0] if side else 1 - flags[0]
+    span = pl.ds(pl.multiple_of(core * half, half), half)
+    for index, weight_ref in enumerate((gate_ref, up_ref)):
+        out_ref[index, 0] = jnp.dot(
+            tokens[...], weight_ref[item, :, span], preferred_element_type=jnp.float32
+        ).astype(out_ref.dtype)
+
+
+def stage_kernel(*refs, first, count):
     half = len(refs) // 2
     sources, targets, sems = refs[:half], refs[half : 2 * half], refs[-1]
-    copies = []
-    for which in range(half):
-        for item in range(sources[which].shape[0]):
-            copies.append(
-                pltpu.make_async_copy(
-                    sources[which].at[item], targets[which].at[item], sems.at[which, item]
-                )
-            )
+    copies = [
+        pltpu.make_async_copy(
+            sources[which].at[first + item], targets[which].at[item], sems.at[which, item]
+        )
+        for item in range(count)
+        for which in range(half)
+    ]
     for copy in copies:
         copy.start()
     for copy in copies:
         copy.wait()
 
 
-def stage(*weights):
+def stage(weights, first, count):
+    shapes = [(count,) + weight.shape[1:] for weight in weights]
+    size = sum(weight[0].size * count for weight in weights)
     return pl.pallas_call(
-        stage_kernel,
-        out_shape=tuple(pltpu.VMEM(weight.shape, weight.dtype) for weight in weights),
+        functools.partial(stage_kernel, first=first, count=count),
+        out_shape=tuple(pltpu.VMEM(shape, weights[0].dtype) for shape in shapes),
         in_specs=[pl.BlockSpec(memory_space=pltpu.HBM)] * len(weights),
         out_specs=(pl.BlockSpec(memory_space=pltpu.VMEM),) * len(weights),
-        scratch_shapes=[pltpu.SemaphoreType.DMA((len(weights), weights[0].shape[0]))],
-        cost_estimate=pl.CostEstimate(
-            flops=0, bytes_accessed=2 * sum(weight.size for weight in weights), transcendentals=0
-        ),
-        compiler_params=pltpu.CompilerParams(vmem_limit_bytes=1024 * 1024),
+        scratch_shapes=[pltpu.SemaphoreType.DMA((len(weights), count))],
+        cost_estimate=pl.CostEstimate(flops=0, bytes_accessed=2 * size, transcendentals=0),
+        compiler_params=pltpu.CompilerParams(vmem_limit_bytes=STAGE_VMEM),
         name="stage",
     )(*weights)
 
 
-def gate_up(parts, flags, w_gate, w_up, first, count):
+def gate_up(parts, flags, w_gate, w_up, side):
     rows = parts[0].shape[0]
-    _, depth, hidden = w_gate.shape
+    count, depth, hidden = w_gate.shape
     half = hidden // 2
-    out_spec = pl.BlockSpec((2, 1, 2 * rows, half), lambda e, j, flags: (0, e, 0, 0))
-    out = jax.ShapeDtypeStruct((2, count, 2 * rows, half), jnp.bfloat16)
     return pl.pallas_call(
-        functools.partial(rows_kernel, parts=len(parts), rows=rows, first=first),
-        out_shape=(out, out),
+        functools.partial(rows_kernel, parts=len(parts), rows=rows, side=side),
+        out_shape=jax.ShapeDtypeStruct((2, count, 2 * rows, half), jnp.bfloat16),
         grid_spec=pltpu.PrefetchScalarGridSpec(
             num_scalar_prefetch=1,
-            grid=(count, 2),
-            in_specs=[pl.BlockSpec((rows, depth), lambda e, j, flags: (0, 0))] * len(parts)
+            grid=(count,),
+            in_specs=[pl.BlockSpec((rows, depth), lambda e, flags: (0, 0))] * len(parts)
             + [pl.BlockSpec(memory_space=pltpu.VMEM)] * 2,
-            out_specs=(out_spec, out_spec),
+            out_specs=pl.BlockSpec((2, 1, 2 * rows, half), lambda e, flags: (0, e, 0, 0)),
             scratch_shapes=[pltpu.VMEM((2 * rows, depth), jnp.bfloat16)],
         ),
         cost_estimate=pl.CostEstimate(
-            flops=8 * rows * depth * hidden * count,
-            bytes_accessed=4 * depth * hidden * count,
+            flops=4 * rows * depth * hidden * count,
+            bytes_accessed=2 * depth * hidden * count,
             transcendentals=0,
         ),
         compiler_params=pltpu.CompilerParams(vmem_limit_bytes=VMEM),
@@ -476,8 +468,7 @@
     kept_ref[...] = part(flags[1])
 
 
-def core_sum(send, keep, flags):
-    got = flip(send, TENSOR, LINE, 1)
+def core_sum(keep, got, flags):
     kinds, count, rows, half = keep.shape
     shape = (kinds, count, rows, half // 2)
     spec = pl.BlockSpec((kinds, 1, rows, half), lambda e, flags: (0, e, 0, 0))
@@ -558,26 +549,32 @@
     w_up,
     w_down,
 ):
+    token_count = layer_input.shape[0]
     local, slice_width, _ = w_gate.shape
     me, side = lax.axis_index(EXPERT), lax.axis_index(TENSOR)
     inner = (me == 1) | (me == 2)
     flags = jnp.stack([side & 1, side >> 1, inner.astype(jnp.int32), me.astype(jnp.int32)])
-    inner, first_core, flags = lax.optimization_barrier((inner, (side & 1) == 0, flags))
+    inner, first_core, first_chip, flags = lax.optimization_barrier(
+        (inner, (side & 1) == 0, (side & 2) == 0, flags)
+    )
     own = expert_rows(layer_input, norm_gain, actual, gates, slice_width, local * LINE)
     pair = lax.ppermute(own, EXPERT, OUTER)
     across = lax.ppermute(own, EXPERT, INNER)
-    blocks = key_blocks(after(kv_latent, own), first_core)
-    gate_near, up_near = stage(*after((w_gate, w_up), own, flags))
-    pair, across, gate_near = after((pair, across, gate_near), gate_near)
+    whole, halves = key_halves(after(kv_latent, own), first_core)
+    step = local // 2
+    early = stage(after((w_gate, w_up), own, flags), 0, step)
+    pair, across, early = after((pair, across, early), early)
     beyond = lax.ppermute(pair, EXPERT, INNER)
     out_first = lax.ppermute(across, EXPERT, OUTWARD)
 
-    step = local // 2
-
-    def turn(parts, index):
-        send, keep = gate_up(parts, flags, gate_near, up_near, index % 2 * step, step)
-        out, kept = core_sum(send, keep, flags)
-        return out, kept, flip(out, TENSOR, 4, 2)
+
+    def turn(parts, weights):
+        send = gate_up(parts, flags, *weights, 0)
+        got = flip(send, TENSOR, LINE, 1)
+        parts = after(parts, send)
+        keep = gate_up(parts, flags, *weights, 1)
+        out, kept = core_sum(keep, got, flags)
+        return out, kept, flip(out, TENSOR, LINE, 2)
 
     def act(kept, got, parts, first):
         return activate(kept, got, parts, flags, first, local, slice_width)
@@ -585,12 +582,13 @@
     def spread_chip(acts):
         return flip(acts, TENSOR, 4, 2)
 
-    out0, kept0, got0 = turn([own, pair], 0)
+    out0, kept0, got0 = turn([own, pair], early)
     out_second = lax.ppermute(beyond, EXPERT, OUTWARD)
+    late = stage(after((w_gate, w_up), out0), step, step)
     near_own, near_pair = after((own, pair), out0, beyond)
-    out1, kept1, got1 = turn([near_own, near_pair], 1)
+    out1, kept1, got1 = turn([near_own, near_pair], late)
     near = [near_own, near_pair]
-    blocks = after(blocks, out1)
+    blocks = key_blocks(whole, after(halves, out1), first_core)
     heads_out = attention(q_absorbed, blocks, w_values, flags)
     across, beyond, out_first, out_second = after(
         (across, beyond, out_first, out_second), heads_out
@@ -598,11 +596,11 @@
     far = [across, beyond, out_first, out_second]
     pair_heads = lax.ppermute(heads_out, EXPERT, OUTER)
     across_heads = lax.ppermute(heads_out, EXPERT, INNER)
-    out2, kept2, got2 = turn(far, 2)
+    out2, kept2, got2 = turn(far, early)
     pair_heads, across_heads, far = after((pair_heads, across_heads, far), out2)
     beyond_heads = lax.ppermute(pair_heads, EXPERT, INNER)
     first_heads = lax.ppermute(across_heads, EXPERT, OUTWARD)
-    out3, kept3, got3 = turn(far, 3)
+    out3, kept3, got3 = turn(far, late)
     beyond_heads, got2, far = after((beyond_heads, got2, far), out3)
     second_heads = lax.ppermute(beyond_heads, EXPERT, OUTWARD)
     act2 = act(kept2, got2, far, 0)
@@ -610,7 +608,7 @@
     got0, got1 = after((got0, got1), act2)
     act0 = act(kept0, got0, near, 0)
     act1 = act(kept1, got1, near, step)
-    (down_near,) = stage(after(w_down, act0, act1))
+    (down_near,) = stage([after(w_down, act0, act1)], 0, local)
     got3 = after(got3, down_near)
     act3 = act(kept3, got3, far, step)
     chip3 = spread_chip(act3)
@@ -634,17 +632,24 @@
     far_pieces = [spread(act2, chip2), spread(act3, chip3)]
     far_first, far_second = down(far_pieces, flags, down_near)
     in_second = lax.ppermute(far_second, EXPERT, INWARD)
-    in_first = lax.ppermute(far_first, EXPERT, INWARD)
-    partial, chip0, chip1 = after((partial, chip0, chip1), far_first)
+    chip0, chip1 = after((chip0, chip1), far_first)
     near_pieces = [spread(act0, chip0), spread(act1, chip1)]
     near_own, near_pair = down(near_pieces, flags, down_near)
+    far_first = after(far_first, near_own)
+    in_first = lax.ppermute(far_first, EXPERT, INWARD)
     got_second = lax.ppermute(add(far_second, in_second), EXPERT, INNER)
     got_first = lax.ppermute(add(far_first, in_first), EXPERT, INNER)
     got_pair = lax.ppermute(add(near_pair, got_second), EXPERT, OUTER)
     mixture = (
         near_own.astype(jnp.float32) + got_first.astype(jnp.float32) + got_pair.astype(jnp.float32)
     ).astype(jnp.bfloat16)
-    mine = halve(partial, TENSOR, 4, 0).astype(jnp.bfloat16)
+    half = 2 * token_count
+    mine = partial
+    for bit, first in ((1, first_core), (2, first_chip)):
+        low, high = mine[:half], mine[half:]
+        got = flip(jnp.where(first, high, low), TENSOR, LINE, bit)
+        mine = add(jnp.where(first, low, high), got)
+        half //= 2
     pairs = []
     for e in range(LINE):
         for t in range(LINE):

time: 267 us -> 268 us (level)
  the two profiles are of different devices: /device:TPU:1 before, /device:TPU:18 now
where the time goes in v1:
time: 268 us; the launch traced here: 267 us
  waiting for transfers between devices  123 us (46%)
  Pallas kernels  70.5 us (26%)
  starting transfers between devices  45.7 us (17%)
  local copies, waits for them, and re-layouts  15.4 us (6%)
  other arithmetic  7.14 us (3%)
  matrix products  4 us (1%)
    ppermute x21, waiting for transfers between devices, flip(): return lax.ppermute(value, axis, [(i, i ^ bit) for i in range(size)])  45.2 us
    pallas_call x8, Pallas kernels, gate_up(): pl.pallas_call(functools.partial(rows_kernel, parts=len(parts), rows=rows...  25.6 us
    pallas_call x3, Pallas kernels, stage(): pl.pallas_call(functools.partial(stage_kernel, first=first, count=count),...  16.3 us
    unnamed x85, local copies, waits for them, and re-layouts  13.6 us
    pallas_call x2, Pallas kernels, down(): pl.pallas_call(functools.partial(down_kernel, counts=counts, rows=rows //...  12.3 us
    ppermute x1, waiting for transfers between devices, layer(): in_second = lax.ppermute(far_second, EXPERT, INWARD)  12 us
    ppermute x1, waiting for transfers between devices, layer(): out_second = lax.ppermute(beyond, EXPERT, OUTWARD)  10.1 us
    ppermute x21, starting transfers between devices, flip(): return lax.ppermute(value, axis, [(i, i ^ bit) for i in range(size)])  9.79 us
  transfers between devices with their start and end apart: 37, of which 20 were waited for; matrix products, arithmetic and copies ran while one was open for 3% of the time, Pallas kernels for 19%

profile of v1, /device:TPU:18, one launch (start us, length us, event | category | flops | bytes accessed | tf_op | source)
XLA Modules:
  0.0 267.1 jit_solution(526195938221904428)
XLA Ops:
  9.5 5.3 %stage.3 = (bf16[2,1792,1024]{2,1,0:T(8,128)(2,1)S(1)}, bf16[2,1792,1024]{2,1,0:T(8,128)(2,1)S(1)}) custom-call(bf16[4,1792,1024]{2,1,0:T(8,128)(2,1)} %refs_0_.1, bf16[4,1792,1024]{2,1,0:T(8,128)(2,1)} %refs_1_.1), custom_call_target="tpu_custom_call" | custom-call | bytes 14680064 | tf_op jit(solution)/shard_map/stage/pallas_call | solution.py:356
  14.8 4.1 %collective-permute-done.2.refs_1_ = bf16[128,1920]{1,0:T(8,128)(2,1)S(1)} collective-permute-done((bf16[128,1920]{1,0:T(8,128)(2,1)S(1)}, bf16[128,1920]{1,0:T(8,128)(2,1)S(1)}, u32[]{:S(2)}, u32[]{:S(2)}) %collective-permute-start.2) | collective-permute-done | bytes 491552 | tf_op jit(solution)/shard_map/ppermute | solution.py:561
  18.8 3.2 %collective-permute-done.3.refs_0_ = bf16[128,1920]{1,0:T(8,128)(2,1)S(1)} collective-permute-done((bf16[128,1920]{1,0:T(8,128)(2,1)S(1)}, bf16[128,1920]{1,0:T(8,128)(2,1)S(1)}, u32[]{:S(2)}, u32[]{:S(2)}) %collective-permute-start.3) | collective-permute-done | bytes 491552 | tf_op jit(solution)/shard_map/ppermute | solution.py:562
  33.3 7.4 %collective-permute-done.5.refs_1_ = bf16[128,1920]{1,0:T(8,128)(2,1)S(1)} collective-permute-done((bf16[128,1920]{1,0:T(8,128)(2,1)S(1)}, bf16[128,1920]{1,0:T(8,128)(2,1)S(1)}, u32[]{:S(2)}, u32[]{:S(2)}) %collective-permute-start.5) | collective-permute-done | bytes 491552 | tf_op jit(solution)/shard_map/ppermute | solution.py:567
  40.7 5.4 %stage.4 = (bf16[2,1792,1024]{2,1,0:T(8,128)(2,1)S(1)}, bf16[2,1792,1024]{2,1,0:T(8,128)(2,1)S(1)}) custom-call(bf16[4,1792,1024]{2,1,0:T(8,128)(2,1)} %refs_0_.1, bf16[4,1792,1024]{2,1,0:T(8,128)(2,1)} %refs_1_.1), custom_call_target="tpu_custom_call" | custom-call | bytes 14680064 | tf_op jit(solution)/shard_map/stage/pallas_call | solution.py:356
  46.2 3.9 %gate_up.10 = bf16[2,2,256,512]{3,2,1,0:T(8,128)(2,1)} custom-call(s32[4]{0:T(128)S(1)} %pad_add_fusion.flags, bf16[128,1920]{1,0:T(8,128)(2,1)S(1)} %copy-done.7, bf16[128,1920]{1,0:T(8,128)(2,1)S(1)} %copy-done.13, bf16[2,1792,1024]{2,1,0:T(8,128)(2,1)S(1)} %get-tuple-element.95.refs_2_.refs_4_, bf16[2,1792,1024]{2,1,0:T(8,128)(2,1)S(1)} %get-tuple-element.96.refs_3_.refs_5_), custom_call_target="tpu_custom_call" | custom-call | flops 1879048192 | bytes 7340032 | tf_op jit(solution)/shard_map/gate_up/pallas_call | solution.py:372
  52.7 4.8 %collective-permute-done = bf16[64,640]{1,0:T(8,128)(2,1)S(1)} collective-permute-done((bf16[64,640]{1,0:T(8,128)(2,1)S(1)}, bf16[64,640]{1,0:T(8,128)(2,1)S(1)}, u32[]{:S(2)}, u32[]{:S(2)}) %collective-permute-start) | collective-permute-done | bytes 81952 | tf_op jit(solution)/shard_map/ppermute | solution.py:52
  57.6 7.1 %collective-permute-done.1 = bf16[2,64,640]{2,1,0:T(8,128)(2,1)S(1)} collective-permute-done((bf16[2,64,640]{2,1,0:T(8,128)(2,1)S(1)}, bf16[2,64,640]{2,1,0:T(8,128)(2,1)S(1)}, u32[]{:S(2)}, u32[]{:S(2)}) %collective-permute-start.1) | collective-permute-done | bytes 163872 | tf_op jit(solution)/shard_map/ppermute | solution.py:52
  78.1 5.9 %collective-permute-start.10 = (bf16[128,1920]{1,0:T(8,128)(2,1)S(1)}, bf16[128,1920]{1,0:T(8,128)(2,1)S(1)}, u32[]{:S(2)}, u32[]{:S(2)}) collective-permute-start(bf16[128,1920]{1,0:T(8,128)(2,1)S(1)} %copy-done.11), channel_id=1, source_target_pairs={{4,0},{8,12},{5,1},{9,13},{6,2},{10,14},{7,3},{11,15},{20,16},{24,... | collective-permute-start | bytes 1474568 | tf_op jit(solution)/shard_map/ppermute | solution.py:568
  86.0 7.2 %attention.1 = bf16[128,2048]{1,0:T(8,128)(2,1)S(1)} custom-call(s32[4]{0:T(128)S(1)} %pad_add_fusion.flags, bf16[128,9216]{1,0:T(8,128)(2,1)S(1)} %copy-done.20, bf16[512,640]{1,0:T(8,128)(2,1)S(1)} %pad_maximum_fusion.even_ref, bf16[512,640]{1,0:T(8,128)(2,1)S(1)} %concatenate.22.odd_ref, bf16[16,512,128]{2,1,0:T(8,128)(2,1)S(1)} %copy-done.21), custom_call_target="tpu_custom_call" | custom-call | flops 2550136832 | bytes 2359296 | tf_op jit(solution)/shard_map/attention/pallas_call | solution.py:264
  95.6 10.1 %collective-permute-done.11.refs_3_ = bf16[128,1920]{1,0:T(8,128)(2,1)S(1)} collective-permute-done((bf16[128,1920]{1,0:T(8,128)(2,1)S(1)}, bf16[128,1920]{1,0:T(8,128)(2,1)S(1)}, u32[]{:S(2)}, u32[]{:S(2)}) %collective-permute-start.11) | collective-permute-done | bytes 491552 | tf_op jit(solution)/shard_map/ppermute | solution.py:586
  105.7 3.1 %gate_up.12 = bf16[2,2,256,512]{3,2,1,0:T(8,128)(2,1)S(1)} custom-call(s32[4]{0:T(128)S(1)} %pad_add_fusion.flags, bf16[128,1920]{1,0:T(8,128)(2,1)S(1)} %copy-done.11, bf16[128,1920]{1,0:T(8,128)(2,1)S(1)} %copy-done.17, bf16[128,1920]{1,0:T(8,128)(2,1)S(1)} %collective-permute-done.10.refs_2_, bf16[128,1920]{1,0:T(8,128)(2,1)S(1)} %collective-permute-done.11.refs_3_, ...), custom_call_target="tpu_custom_call" | custom-call | flops 1879048192 | bytes 7340032 | tf_op jit(solution)/shard_map/gate_up/pallas_call | solution.py:372
  113.7 3.1 %gate_up.13.keep_ref = bf16[2,2,256,512]{3,2,1,0:T(8,128)(2,1)S(1)} custom-call(s32[4]{0:T(128)S(1)} %pad_add_fusion.flags, bf16[128,1920]{1,0:T(8,128)(2,1)S(1)} %copy-done.11, bf16[128,1920]{1,0:T(8,128)(2,1)S(1)} %copy-done.17, bf16[128,1920]{1,0:T(8,128)(2,1)S(1)} %collective-permute-done.10.refs_2_, ...), custom_call_target="tpu_custom_call" | custom-call | flops 1879048192 | bytes 7340032 | tf_op jit(solution)/shard_map/gate_up/pallas_call | solution.py:372
  117.9 6.1 %collective-permute-done.8 = bf16[128,2048]{1,0:T(8,128)(2,1)S(1)} collective-permute-done((bf16[128,2048]{1,0:T(8,128)(2,1)S(1)}, bf16[128,2048]{1,0:T(8,128)(2,1)S(1)}, u32[]{:S(2)}, u32[]{:S(2)}) %collective-permute-start.8) | collective-permute-done | bytes 524320 | tf_op jit(solution)/shard_map/ppermute | solution.py:597
  124.0 3.3 %collective-permute-done.9 = bf16[128,2048]{1,0:T(8,128)(2,1)S(1)} collective-permute-done((bf16[128,2048]{1,0:T(8,128)(2,1)S(1)}, bf16[128,2048]{1,0:T(8,128)(2,1)S(1)}, u32[]{:S(2)}, u32[]{:S(2)}) %collective-permute-start.9) | collective-permute-done | bytes 524320 | tf_op jit(solution)/shard_map/ppermute | solution.py:598
  135.6 3.1 %gate_up.15.keep_ref = bf16[2,2,256,512]{3,2,1,0:T(8,128)(2,1)S(1)} custom-call(s32[4]{0:T(128)S(1)} %pad_add_fusion.flags, bf16[128,1920]{1,0:T(8,128)(2,1)S(1)} %copy-done.11, bf16[128,1920]{1,0:T(8,128)(2,1)S(1)} %copy-done.17, bf16[128,1920]{1,0:T(8,128)(2,1)S(1)} %collective-permute-done.10.refs_2_, ...), custom_call_target="tpu_custom_call" | custom-call | flops 1879048192 | bytes 7340032 | tf_op jit(solution)/shard_map/gate_up/pallas_call | solution.py:372
  141.5 5.4 %collective-permute-done.14 = bf16[128,2048]{1,0:T(8,128)(2,1)S(1)} collective-permute-done((bf16[128,2048]{1,0:T(8,128)(2,1)S(1)}, bf16[128,2048]{1,0:T(8,128)(2,1)S(1)}, u32[]{:S(2)}, u32[]{:S(2)}) %collective-permute-start.14) | collective-permute-done | bytes 524320 | tf_op jit(solution)/shard_map/ppermute | solution.py:601
  150.5 8.6 %collective-permute-done.19.got_ref = bf16[2,2,256,256]{3,2,1,0:T(8,128)(2,1)S(1)} collective-permute-done((bf16[2,2,256,256]{3,2,1,0:T(8,128)(2,1)S(1)}, bf16[2,2,256,256]{3,2,1,0:T(8,128)(2,1)S(1)}, u32[]{:S(2)}, u32[]{:S(2)}) %collective-permute-start.19) | collective-permute-done | bytes 524320 | tf_op jit(solution)/shard_map/ppermute | solution.py:52
  159.7 10.7 %collective-permute-done.20.got_ref = bf16[2,2,256,256]{3,2,1,0:T(8,128)(2,1)S(1)} collective-permute-done((bf16[2,2,256,256]{3,2,1,0:T(8,128)(2,1)S(1)}, bf16[2,2,256,256]{3,2,1,0:T(8,128)(2,1)S(1)}, u32[]{:S(2)}, u32[]{:S(2)}) %collective-permute-start.20) | collective-permute-done | bytes 524320 | tf_op jit(solution)/shard_map/ppermute | solution.py:52
  172.3 5.5 %stage.5.refs_4_ = bf16[4,1024,1792]{2,1,0:T(8,128)(2,1)S(1)} custom-call(bf16[4,1024,1792]{2,1,0:T(8,128)(2,1)} %refs_0_.2), custom_call_target="tpu_custom_call" | custom-call | bytes 14680064 | tf_op jit(solution)/shard_map/stage/pallas_call | solution.py:356
  177.9 3.7 %collective-permute-done.18.got_ref = bf16[2,2,256,256]{3,2,1,0:T(8,128)(2,1)S(1)} collective-permute-done((bf16[2,2,256,256]{3,2,1,0:T(8,128)(2,1)S(1)}, bf16[2,2,256,256]{3,2,1,0:T(8,128)(2,1)S(1)}, u32[]{:S(2)}, u32[]{:S(2)}) %collective-permute-start.18) | collective-permute-done | bytes 524320 | tf_op jit(solution)/shard_map/ppermute | solution.py:52
  183.8 4.0 %convolution_convert_fusion = bf16[512,1792]{1,0:T(8,128)(2,1)S(1)} fusion(bf16[2048,1792]{1,0:T(8,128)(2,1)S(1)} %bitcast.43, bf16[128,2048]{1,0:T(8,128)(2,1)S(1)} %get-tuple-element.156, bf16[128,2048]{1,0:T(8,128)(2,1)S(1)} %get-tuple-element.157, bf16[128,2048]{1,0:T(8,128)(2,1)S(1)} %copy-done.31, bf16[128,2048]{1,0:T(8,128)(2,1)S(1)} %copy-done.25), kind=kOutput, calls=%fused_computation.1 | convolution fusion | flops 3767402496 | bytes 11272192 | tf_op jit(solution)/shard_map/dot_general | solution.py:630
  187.8 4.2 %collective-permute-done.27 = bf16[2,256,256]{2,1,0:T(8,128)(2,1)S(1)} collective-permute-done((bf16[2,256,256]{2,1,0:T(8,128)(2,1)S(1)}, bf16[2,256,256]{2,1,0:T(8,128)(2,1)S(1)}, u32[]{:S(2)}, u32[]{:S(2)}) %collective-permute-start.27) | collective-permute-done | bytes 262176 | tf_op jit(solution)/shard_map/ppermute | solution.py:52
  195.1 6.2 %down.2 = (bf16[128,1792]{1,0:T(8,128)(2,1)S(1)}, bf16[128,1792]{1,0:T(8,128)(2,1)S(1)}) custom-call(s32[4]{0:T(128)S(1)} %pad_add_fusion.flags, bf16[2,2,256,256]{3,2,1,0:T(8,128)(2,1)S(1)} %pad_maximum_fusion.1.refs_0_, bf16[2,2,256,256]{3,2,1,0:T(8,128)(2,1)S(1)} %collective-permute-done.28.refs_1_, ...), custom_call_target="tpu_custom_call" | custom-call | flops 3758096384 | bytes 14680064 | tf_op jit(solution)/shard_map/down/pallas_call | solution.py:438
  202.2 5.1 %collective-permute-done.25 = bf16[2,256,256]{2,1,0:T(8,128)(2,1)S(1)} collective-permute-done((bf16[2,256,256]{2,1,0:T(8,128)(2,1)S(1)}, bf16[2,256,256]{2,1,0:T(8,128)(2,1)S(1)}, u32[]{:S(2)}, u32[]{:S(2)}) %collective-permute-start.25) | collective-permute-done | bytes 262176 | tf_op jit(solution)/shard_map/ppermute | solution.py:52
  210.4 12.0 %collective-permute-done.34 = bf16[128,1792]{1,0:T(8,128)(2,1)S(1)} collective-permute-done((bf16[128,1792]{1,0:T(8,128)(2,1)S(1)}, bf16[128,1792]{1,0:T(8,128)(2,1)S(1)}, u32[]{:S(2)}, u32[]{:S(2)}) %collective-permute-start.34) | collective-permute-done | bytes 458784 | tf_op jit(solution)/shard_map/ppermute | solution.py:634
  222.5 3.6 %collective-permute-start.35 = (bf16[128,1792]{1,0:T(8,128)(2,1)S(1)}, bf16[128,1792]{1,0:T(8,128)(2,1)S(1)}, u32[]{:S(2)}, u32[]{:S(2)}) collective-permute-start(bf16[128,1792]{1,0:T(8,128)(2,1)S(1)} %add_convert_fusion.3), channel_id=1, source_target_pairs={{4,8},{8,4},{5,9},{9,5},{6,10},{10,6},{7,11},{11,7},{20,24},{24,20... | collective-permute-start | bytes 1376264 | tf_op jit(solution)/shard_map/ppermute | solution.py:640
  226.2 6.2 %down.3 = (bf16[128,1792]{1,0:T(8,128)(2,1)S(1)}, bf16[128,1792]{1,0:T(8,128)(2,1)S(1)}) custom-call(s32[4]{0:T(128)S(1)} %pad_add_fusion.flags, bf16[2,2,256,256]{3,2,1,0:T(8,128)(2,1)S(1)} %pad_maximum_fusion.3.refs_0_, bf16[2,2,256,256]{3,2,1,0:T(8,128)(2,1)S(1)} %collective-permute-done.30.refs_1_, ...), custom_call_target="tpu_custom_call" | custom-call | flops 3758096384 | bytes 14680064 | tf_op jit(solution)/shard_map/down/pallas_call | solution.py:438
  234.0 4.6 %collective-permute-start.23 = (bf16[128,1792]{1,0:T(8,128)(2,1)S(1)}, bf16[128,1792]{1,0:T(8,128)(2,1)S(1)}, u32[]{:S(2)}, u32[]{:S(2)}) collective-permute-start(bf16[128,1792]{1,0:T(8,128)(2,1)S(1)} %add_convert_fusion.5), channel_id=1, source_target_pairs={{0,0},{1,8},{2,4},{3,12},{4,5},{5,9},{6,1},{7,13},{8,10},{9,6},{10... | collective-permute-start | bytes 1376264 | tf_op jit(solution)/shard_map/ppermute | solution.py:658
  238.8 8.9 %collective-permute-done.32 = bf16[128,1792]{1,0:T(8,128)(2,1)S(1)} collective-permute-done((bf16[128,1792]{1,0:T(8,128)(2,1)S(1)}, bf16[128,1792]{1,0:T(8,128)(2,1)S(1)}, u32[]{:S(2)}, u32[]{:S(2)}) %collective-permute-start.32) | collective-permute-done | bytes 458784 | tf_op jit(solution)/shard_map/ppermute | solution.py:639
  250.7 7.2 %collective-permute-done.23 = bf16[128,1792]{1,0:T(8,128)(2,1)S(1)} collective-permute-done((bf16[128,1792]{1,0:T(8,128)(2,1)S(1)}, bf16[128,1792]{1,0:T(8,128)(2,1)S(1)}, u32[]{:S(2)}, u32[]{:S(2)}) %collective-permute-start.23) | collective-permute-done | bytes 458784 | tf_op jit(solution)/shard_map/ppermute | solution.py:658
  257.9 7.5 %collective-permute-done.36 = bf16[128,1792]{1,0:T(8,128)(2,1)S(1)} collective-permute-done((bf16[128,1792]{1,0:T(8,128)(2,1)S(1)}, bf16[128,1792]{1,0:T(8,128)(2,1)S(1)}, u32[]{:S(2)}, u32[]{:S(2)}) %collective-permute-start.36) | collective-permute-done | bytes 458784 | tf_op jit(solution)/shard_map/ppermute | solution.py:642
  (193 shorter events, 78.9 us)
Async XLA Ops:
  5.8 13.0 %collective-permute-start.2 = (bf16[128,1920]{1,0:T(8,128)(2,1)S(1)}, bf16[128,1920]{1,0:T(8,128)(2,1)S(1)}, u32[]{:S(2)}, u32[]{:S(2)}) collective-permute-start(bf16[128,1920]{1,0:T(8,128)(2,1)S(1)} %concatenate.18.refs_0_), channel_id=1, source_target_pairs={{0,4},{4,0},{8,12},{12,8},{1,5},{5,1},{9,13},{13,9},{2,6},{6,2},{1... | collective-permute-start | bytes 1474568 | tf_op jit(solution)/shard_map/ppermute | solution.py:561
  7.4 14.6 %collective-permute-start.3 = (bf16[128,1920]{1,0:T(8,128)(2,1)S(1)}, bf16[128,1920]{1,0:T(8,128)(2,1)S(1)}, u32[]{:S(2)}, u32[]{:S(2)}) collective-permute-start(bf16[128,1920]{1,0:T(8,128)(2,1)S(1)} %concatenate.18.refs_0_), channel_id=1, source_target_pairs={{4,8},{8,4},{5,9},{9,5},{6,10},{10,6},{7,11},{11,7},{20,24},{24,20... | collective-permute-start | bytes 1474568 | tf_op jit(solution)/shard_map/ppermute | solution.py:562
  25.2 15.5 %collective-permute-start.5 = (bf16[128,1920]{1,0:T(8,128)(2,1)S(1)}, bf16[128,1920]{1,0:T(8,128)(2,1)S(1)}, u32[]{:S(2)}, u32[]{:S(2)}) collective-permute-start(bf16[128,1920]{1,0:T(8,128)(2,1)S(1)} %collective-permute-done.2.refs_1_), channel_id=1, source_target_pairs={{4,8},{8,4},{5,9},{9,5},{6,10},{10,6},{7,11},{11,7},{20,24},{24,20... | collective-permute-start | bytes 1474568 | tf_op jit(solution)/shard_map/ppermute | solution.py:567
  52.4 23.6 %collective-permute-start.6 = (bf16[2,2,256,512]{3,2,1,0:T(8,128)(2,1)}, bf16[2,2,256,512]{3,2,1,0:T(8,128)(2,1)}, u32[]{:S(2)}, u32[]{:S(2)}) collective-permute-start(bf16[2,2,256,512]{3,2,1,0:T(8,128)(2,1)} %gate_up.10), channel_id=1, source_target_pairs={{0,1},{1,0},{2,3},{3,2},{4,5},{5,4},{6,7},{7,6},{8,9},{9,8},{10,11... | collective-permute-start | bytes 3145736 | tf_op jit(solution)/shard_map/ppermute | solution.py:52
  78.0 7.4 %collective-permute-start.7 = (bf16[3,64,640]{2,1,0:T(8,128)(2,1)S(1)}, bf16[3,64,640]{2,1,0:T(8,128)(2,1)S(1)}, u32[]{:S(2)}, u32[]{:S(2)}) collective-permute-start(bf16[3,64,640]{2,1,0:T(8,128)(2,1)S(1)} %pad_maximum_fusion.5), channel_id=1, source_target_pairs={{0,1},{1,0},{2,3},{3,2},{4,5},{5,4},{6,7},{7,6},{8,9},{9,8},{10,11... | collective-permute-start | bytes 737288 | tf_op jit(solution)/shard_map/ppermute | solution.py:52
  78.1 17.4 %collective-permute-start.10 = (bf16[128,1920]{1,0:T(8,128)(2,1)S(1)}, bf16[128,1920]{1,0:T(8,128)(2,1)S(1)}, u32[]{:S(2)}, u32[]{:S(2)}) collective-permute-start(bf16[128,1920]{1,0:T(8,128)(2,1)S(1)} %copy-done.11), channel_id=1, source_target_pairs={{4,0},{8,12},{5,1},{9,13},{6,2},{10,14},{7,3},{11,15},{20,16},{24,... | collective-permute-start | bytes 1474568 | tf_op jit(solution)/shard_map/ppermute | solution.py:568
  84.0 21.6 %collective-permute-start.11 = (bf16[128,1920]{1,0:T(8,128)(2,1)S(1)}, bf16[128,1920]{1,0:T(8,128)(2,1)S(1)}, u32[]{:S(2)}, u32[]{:S(2)}) collective-permute-start(bf16[128,1920]{1,0:T(8,128)(2,1)S(1)} %copy-done.17), channel_id=1, source_target_pairs={{4,0},{8,12},{5,1},{9,13},{6,2},{10,14},{7,3},{11,15},{20,16},{24,... | collective-permute-start | bytes 1474568 | tf_op jit(solution)/shard_map/ppermute | solution.py:586
  108.9 8.0 %collective-permute-start.12 = (bf16[2,2,256,512]{3,2,1,0:T(8,128)(2,1)S(1)}, bf16[2,2,256,512]{3,2,1,0:T(8,128)(2,1)S(1)}, u32[]{:S(2)}, u32[]{:S(2)}) collective-permute-start(bf16[2,2,256,512]{3,2,1,0:T(8,128)(2,1)S(1)} %gate_up.12), channel_id=1, source_target_pairs={{0,1},{1,0},{2,3},{3,2},{4,5},{5,4},{6,7},{7,6},{8,9},{9,8},{10,11... | collective-permute-start | bytes 3145736 | tf_op jit(solution)/shard_map/ppermute | solution.py:52
  108.9 15.1 %collective-permute-start.8 = (bf16[128,2048]{1,0:T(8,128)(2,1)S(1)}, bf16[128,2048]{1,0:T(8,128)(2,1)S(1)}, u32[]{:S(2)}, u32[]{:S(2)}) collective-permute-start(bf16[128,2048]{1,0:T(8,128)(2,1)S(1)} %attention.1), channel_id=1, source_target_pairs={{0,4},{4,0},{8,12},{12,8},{1,5},{5,1},{9,13},{13,9},{2,6},{6,2},{1... | collective-permute-start | bytes 1572872 | tf_op jit(solution)/shard_map/ppermute | solution.py:597
  111.5 15.9 %collective-permute-start.9 = (bf16[128,2048]{1,0:T(8,128)(2,1)S(1)}, bf16[128,2048]{1,0:T(8,128)(2,1)S(1)}, u32[]{:S(2)}, u32[]{:S(2)}) collective-permute-start(bf16[128,2048]{1,0:T(8,128)(2,1)S(1)} %attention.1), channel_id=1, source_target_pairs={{4,8},{8,4},{5,9},{9,5},{6,10},{10,6},{7,11},{11,7},{20,24},{24,20... | collective-permute-start | bytes 1572872 | tf_op jit(solution)/shard_map/ppermute | solution.py:598
  130.5 8.2 %collective-permute-start.16 = (bf16[2,2,256,512]{3,2,1,0:T(8,128)(2,1)S(1)}, bf16[2,2,256,512]{3,2,1,0:T(8,128)(2,1)S(1)}, u32[]{:S(2)}, u32[]{:S(2)}) collective-permute-start(bf16[2,2,256,512]{3,2,1,0:T(8,128)(2,1)S(1)} %gate_up.14), channel_id=1, source_target_pairs={{0,1},{1,0},{2,3},{3,2},{4,5},{5,4},{6,7},{7,6},{8,9},{9,8},{10,11... | collective-permute-start | bytes 3145736 | tf_op jit(solution)/shard_map/ppermute | solution.py:52
  130.6 16.2 %collective-permute-start.14 = (bf16[128,2048]{1,0:T(8,128)(2,1)S(1)}, bf16[128,2048]{1,0:T(8,128)(2,1)S(1)}, u32[]{:S(2)}, u32[]{:S(2)}) collective-permute-start(bf16[128,2048]{1,0:T(8,128)(2,1)S(1)} %collective-permute-done.8), channel_id=1, source_target_pairs={{4,8},{8,4},{5,9},{9,5},{6,10},{10,6},{7,11},{11,7},{20,24},{24,20... | collective-permute-start | bytes 1572872 | tf_op jit(solution)/shard_map/ppermute | solution.py:601
  133.0 15.1 %collective-permute-start.15 = (bf16[2,2,256,256]{3,2,1,0:T(8,128)(2,1)S(1)}, bf16[2,2,256,256]{3,2,1,0:T(8,128)(2,1)S(1)}, u32[]{:S(2)}, u32[]{:S(2)}) collective-permute-start(bf16[2,2,256,256]{3,2,1,0:T(8,128)(2,1)S(1)} %get-tuple-element.110), channel_id=1, source_target_pairs={{0,2},{1,3},{2,0},{3,1},{4,6},{5,7},{6,4},{7,5},{8,10},{9,11},{10,... | collective-permute-start | bytes 1572872 | tf_op jit(solution)/shard_map/ppermute | solution.py:52
  133.6 25.5 %collective-permute-start.19 = (bf16[2,2,256,256]{3,2,1,0:T(8,128)(2,1)S(1)}, bf16[2,2,256,256]{3,2,1,0:T(8,128)(2,1)S(1)}, u32[]{:S(2)}, u32[]{:S(2)}) collective-permute-start(bf16[2,2,256,256]{3,2,1,0:T(8,128)(2,1)S(1)} %copy-done.23), channel_id=1, source_target_pairs={{0,2},{1,3},{2,0},{3,1},{4,6},{5,7},{6,4},{7,5},{8,10},{9,11},{10,... | collective-permute-start | bytes 1572872 | tf_op jit(solution)/shard_map/ppermute | solution.py:52
  135.1 35.2 %collective-permute-start.20 = (bf16[2,2,256,256]{3,2,1,0:T(8,128)(2,1)S(1)}, bf16[2,2,256,256]{3,2,1,0:T(8,128)(2,1)S(1)}, u32[]{:S(2)}, u32[]{:S(2)}) collective-permute-start(bf16[2,2,256,256]{3,2,1,0:T(8,128)(2,1)S(1)} %get-tuple-element.99), channel_id=1, source_target_pairs={{0,2},{1,3},{2,0},{3,1},{4,6},{5,7},{6,4},{7,5},{8,10},{9,11},{10,... | collective-permute-start | bytes 1572872 | tf_op jit(solution)/shard_map/ppermute | solution.py:52
  139.9 41.7 %collective-permute-start.18 = (bf16[2,2,256,256]{3,2,1,0:T(8,128)(2,1)S(1)}, bf16[2,2,256,256]{3,2,1,0:T(8,128)(2,1)S(1)}, u32[]{:S(2)}, u32[]{:S(2)}) collective-permute-start(bf16[2,2,256,256]{3,2,1,0:T(8,128)(2,1)S(1)} %get-tuple-element.122), channel_id=1, source_target_pairs={{0,2},{1,3},{2,0},{3,1},{4,6},{5,7},{6,4},{7,5},{8,10},{9,11},{10,... | collective-permute-start | bytes 1572872 | tf_op jit(solution)/shard_map/ppermute | solution.py:52
  146.8 36.4 %collective-permute-start.13 = (bf16[128,2048]{1,0:T(8,128)(2,1)S(1)}, bf16[128,2048]{1,0:T(8,128)(2,1)S(1)}, u32[]{:S(2)}, u32[]{:S(2)}) collective-permute-start(bf16[128,2048]{1,0:T(8,128)(2,1)S(1)} %collective-permute-done.9), channel_id=1, source_target_pairs={{4,0},{8,12},{5,1},{9,13},{6,2},{10,14},{7,3},{11,15},{20,16},{24,... | collective-permute-start | bytes 1572872 | tf_op jit(solution)/shard_map/ppermute | solution.py:602
  148.2 35.1 %collective-permute-start.17 = (bf16[128,2048]{1,0:T(8,128)(2,1)S(1)}, bf16[128,2048]{1,0:T(8,128)(2,1)S(1)}, u32[]{:S(2)}, u32[]{:S(2)}) collective-permute-start(bf16[128,2048]{1,0:T(8,128)(2,1)S(1)} %collective-permute-done.14), channel_id=1, source_target_pairs={{4,0},{8,12},{5,1},{9,13},{6,2},{10,14},{7,3},{11,15},{20,16},{24,... | collective-permute-start | bytes 1572872 | tf_op jit(solution)/shard_map/ppermute | solution.py:605
  159.1 28.7 %collective-permute-start.26 = (bf16[2,256,256]{2,1,0:T(8,128)(2,1)S(1)}, bf16[2,256,256]{2,1,0:T(8,128)(2,1)S(1)}, u32[]{:S(2)}, u32[]{:S(2)}) collective-permute-start(bf16[2,256,256]{2,1,0:T(8,128)(2,1)S(1)} %activate.4), channel_id=1, source_target_pairs={{0,2},{1,3},{2,0},{3,1},{4,6},{5,7},{6,4},{7,5},{8,10},{9,11},{10,... | collective-permute-start | bytes 786440 | tf_op jit(solution)/shard_map/ppermute | solution.py:52
  182.6 9.4 %collective-permute-start.27 = (bf16[2,256,256]{2,1,0:T(8,128)(2,1)S(1)}, bf16[2,256,256]{2,1,0:T(8,128)(2,1)S(1)}, u32[]{:S(2)}, u32[]{:S(2)}) collective-permute-start(bf16[2,256,256]{2,1,0:T(8,128)(2,1)S(1)} %activate.7), channel_id=1, source_target_pairs={{0,2},{1,3},{2,0},{3,1},{4,6},{5,7},{6,4},{7,5},{8,10},{9,11},{10,... | collective-permute-start | bytes 786440 | tf_op jit(solution)/shard_map/ppermute | solution.py:52
  192.9 16.4 %collective-permute-start.21 = (bf16[256,1792]{1,0:T(8,128)(2,1)S(1)}, bf16[256,1792]{1,0:T(8,128)(2,1)S(1)}, u32[]{:S(2)}, u32[]{:S(2)}) collective-permute-start(bf16[256,1792]{1,0:T(8,128)(2,1)S(1)} %broadcast_select_fusion), channel_id=1, source_target_pairs={{0,1},{1,0},{2,3},{3,2},{4,5},{5,4},{6,7},{7,6},{8,9},{9,8},{10,11... | collective-permute-start | bytes 2752520 | tf_op jit(solution)/shard_map/ppermute | solution.py:52
  193.0 9.2 %collective-permute-start.24 = (bf16[2,256,256]{2,1,0:T(8,128)(2,1)S(1)}, bf16[2,256,256]{2,1,0:T(8,128)(2,1)S(1)}, u32[]{:S(2)}, u32[]{:S(2)}) collective-permute-start(bf16[2,256,256]{2,1,0:T(8,128)(2,1)S(1)} %activate.5), channel_id=1, source_target_pairs={{0,2},{1,3},{2,0},{3,1},{4,6},{5,7},{6,4},{7,5},{8,10},{9,11},{10,... | collective-permute-start | bytes 786440 | tf_op jit(solution)/shard_map/ppermute | solution.py:52
  193.6 13.7 %collective-permute-start.25 = (bf16[2,256,256]{2,1,0:T(8,128)(2,1)S(1)}, bf16[2,256,256]{2,1,0:T(8,128)(2,1)S(1)}, u32[]{:S(2)}, u32[]{:S(2)}) collective-permute-start(bf16[2,256,256]{2,1,0:T(8,128)(2,1)S(1)} %activate.6), channel_id=1, source_target_pairs={{0,2},{1,3},{2,0},{3,1},{4,6},{5,7},{6,4},{7,5},{8,10},{9,11},{10,... | collective-permute-start | bytes 786440 | tf_op jit(solution)/shard_map/ppermute | solution.py:52
  207.4 18.8 %collective-permute-start.31 = (bf16[2,2,256,256]{3,2,1,0:T(8,128)(2,1)S(1)}, bf16[2,2,256,256]{3,2,1,0:T(8,128)(2,1)S(1)}, u32[]{:S(2)}, u32[]{:S(2)}) collective-permute-start(bf16[2,2,256,256]{3,2,1,0:T(8,128)(2,1)S(1)} %pad_maximum_fusion.4.refs_2_), channel_id=1, source_target_pairs={{0,1},{1,0},{2,3},{3,2},{4,5},{5,4},{6,7},{7,6},{8,9},{9,8},{10,11... | collective-permute-start | bytes 1572872 | tf_op jit(solution)/shard_map/ppermute | solution.py:52
  207.5 18.7 %collective-permute-start.30 = (bf16[2,2,256,256]{3,2,1,0:T(8,128)(2,1)S(1)}, bf16[2,2,256,256]{3,2,1,0:T(8,128)(2,1)S(1)}, u32[]{:S(2)}, u32[]{:S(2)}) collective-permute-start(bf16[2,2,256,256]{3,2,1,0:T(8,128)(2,1)S(1)} %pad_maximum_fusion.3.refs_0_), channel_id=1, source_target_pairs={{0,1},{1,0},{2,3},{3,2},{4,5},{5,4},{6,7},{7,6},{8,9},{9,8},{10,11... | collective-permute-start | bytes 1572872 | tf_op jit(solution)/shard_map/ppermute | solution.py:52
  208.1 14.3 %collective-permute-start.34 = (bf16[128,1792]{1,0:T(8,128)(2,1)S(1)}, bf16[128,1792]{1,0:T(8,128)(2,1)S(1)}, u32[]{:S(2)}, u32[]{:S(2)}) collective-permute-start(bf16[128,1792]{1,0:T(8,128)(2,1)S(1)} %get-tuple-element.150), channel_id=1, source_target_pairs={{0,4},{12,8},{1,5},{13,9},{2,6},{14,10},{3,7},{15,11},{16,20},{28,... | collective-permute-start | bytes 1376264 | tf_op jit(solution)/shard_map/ppermute | solution.py:634
  209.8 24.0 %collective-permute-start.22 = (bf16[128,1792]{1,0:T(8,128)(2,1)S(1)}, bf16[128,1792]{1,0:T(8,128)(2,1)S(1)}, u32[]{:S(2)}, u32[]{:S(2)}) collective-permute-start(bf16[128,1792]{1,0:T(8,128)(2,1)S(1)} %broadcast_select_fusion.3), channel_id=1, source_target_pairs={{0,2},{1,3},{2,0},{3,1},{4,6},{5,7},{6,4},{7,5},{8,10},{9,11},{10,... | collective-permute-start | bytes 1376264 | tf_op jit(solution)/shard_map/ppermute | solution.py:52
  222.5 16.1 %collective-permute-start.35 = (bf16[128,1792]{1,0:T(8,128)(2,1)S(1)}, bf16[128,1792]{1,0:T(8,128)(2,1)S(1)}, u32[]{:S(2)}, u32[]{:S(2)}) collective-permute-start(bf16[128,1792]{1,0:T(8,128)(2,1)S(1)} %add_convert_fusion.3), channel_id=1, source_target_pairs={{4,8},{8,4},{5,9},{9,5},{6,10},{10,6},{7,11},{11,7},{20,24},{24,20... | collective-permute-start | bytes 1376264 | tf_op jit(solution)/shard_map/ppermute | solution.py:640
  232.4 15.4 %collective-permute-start.32 = (bf16[128,1792]{1,0:T(8,128)(2,1)S(1)}, bf16[128,1792]{1,0:T(8,128)(2,1)S(1)}, u32[]{:S(2)}, u32[]{:S(2)}) collective-permute-start(bf16[128,1792]{1,0:T(8,128)(2,1)S(1)} %get-tuple-element.148), channel_id=1, source_target_pairs={{0,4},{12,8},{1,5},{13,9},{2,6},{14,10},{3,7},{15,11},{16,20},{28,... | collective-permute-start | bytes 1376264 | tf_op jit(solution)/shard_map/ppermute | solution.py:639
  234.0 23.8 %collective-permute-start.23 = (bf16[128,1792]{1,0:T(8,128)(2,1)S(1)}, bf16[128,1792]{1,0:T(8,128)(2,1)S(1)}, u32[]{:S(2)}, u32[]{:S(2)}) collective-permute-start(bf16[128,1792]{1,0:T(8,128)(2,1)S(1)} %add_convert_fusion.5), channel_id=1, source_target_pairs={{0,0},{1,8},{2,4},{3,12},{4,5},{5,9},{6,1},{7,13},{8,10},{9,6},{10... | collective-permute-start | bytes 1376264 | tf_op jit(solution)/shard_map/ppermute | solution.py:658
  238.8 26.6 %collective-permute-start.36 = (bf16[128,1792]{1,0:T(8,128)(2,1)S(1)}, bf16[128,1792]{1,0:T(8,128)(2,1)S(1)}, u32[]{:S(2)}, u32[]{:S(2)}) collective-permute-start(bf16[128,1792]{1,0:T(8,128)(2,1)S(1)} %add_convert_fusion.2), channel_id=1, source_target_pairs={{0,4},{4,0},{8,12},{12,8},{1,5},{5,1},{9,13},{13,9},{2,6},{6,2},{1... | collective-permute-start | bytes 1376264 | tf_op jit(solution)/shard_map/ppermute | solution.py:642
  247.9 17.5 %collective-permute-start.33 = (bf16[128,1792]{1,0:T(8,128)(2,1)S(1)}, bf16[128,1792]{1,0:T(8,128)(2,1)S(1)}, u32[]{:S(2)}, u32[]{:S(2)}) collective-permute-start(bf16[128,1792]{1,0:T(8,128)(2,1)S(1)} %add_convert_fusion.4), channel_id=1, source_target_pairs={{4,8},{8,4},{5,9},{9,5},{6,10},{10,6},{7,11},{11,7},{20,24},{24,20... | collective-permute-start | bytes 1376264 | tf_op jit(solution)/shard_map/ppermute | solution.py:641
  (47 other events, 569.3 us)

commit v2 on v1

--- a/solution.py
+++ b/solution.py
@@ -563,30 +563,29 @@
     whole, halves = key_halves(after(kv_latent, own), first_core)
     step = local // 2
     early = stage(after((w_gate, w_up), own, flags), 0, step)
-    pair, across, early = after((pair, across, early), early)
-    beyond = lax.ppermute(pair, EXPERT, INNER)
-    out_first = lax.ppermute(across, EXPERT, OUTWARD)
-
-
-    def turn(parts, weights):
+    pair, early = after((pair, early), early)
+
+    def act(kept, got, parts, first):
+        return activate(kept, got, parts, flags, first, local, slice_width)
+
+    def turn(parts, weights, pending=()):
         send = gate_up(parts, flags, *weights, 0)
         got = flip(send, TENSOR, LINE, 1)
-        parts = after(parts, send)
+        parts, pending = after((parts, pending), send)
         keep = gate_up(parts, flags, *weights, 1)
         out, kept = core_sum(keep, got, flags)
-        return out, kept, flip(out, TENSOR, LINE, 2)
-
-    def act(kept, got, parts, first):
-        return activate(kept, got, parts, flags, first, local, slice_width)
+        return (out, kept, flip(out, TENSOR, LINE, 2)), pending
 
     def spread_chip(acts):
-        return flip(acts, TENSOR, 4, 2)
-
-    out0, kept0, got0 = turn([own, pair], early)
+        return flip(acts, TENSOR, LINE, 2)
+
+    (out0, kept0, got0), (pair_on, across) = turn([own, pair], early, (pair, across))
+    beyond = lax.ppermute(pair_on, EXPERT, INNER)
+    out_first = lax.ppermute(across, EXPERT, OUTWARD)
+    late = stage(after((w_gate, w_up), out0), step, step)
+    near_own, near_pair, beyond = after((own, pair, beyond), late)
     out_second = lax.ppermute(beyond, EXPERT, OUTWARD)
-    late = stage(after((w_gate, w_up), out0), step, step)
-    near_own, near_pair = after((own, pair), out0, beyond)
-    out1, kept1, got1 = turn([near_own, near_pair], late)
+    (out1, kept1, got1), _ = turn([near_own, near_pair], late)
     near = [near_own, near_pair]
     blocks = key_blocks(whole, after(halves, out1), first_core)
     heads_out = attention(q_absorbed, blocks, w_values, flags)
@@ -596,27 +595,30 @@
     far = [across, beyond, out_first, out_second]
     pair_heads = lax.ppermute(heads_out, EXPERT, OUTER)
     across_heads = lax.ppermute(heads_out, EXPERT, INNER)
-    out2, kept2, got2 = turn(far, early)
-    pair_heads, across_heads, far = after((pair_heads, across_heads, far), out2)
+    (out2, kept2, got2), _ = turn(far, early)
+    far = after(far, out2)
+    (out3, kept3, got3), _ = turn(far, late)
+    pair_heads, across_heads, got2, far = after((pair_heads, across_heads, got2, far), out3)
     beyond_heads = lax.ppermute(pair_heads, EXPERT, INNER)
     first_heads = lax.ppermute(across_heads, EXPERT, OUTWARD)
-    out3, kept3, got3 = turn(far, late)
-    beyond_heads, got2, far = after((beyond_heads, got2, far), out3)
-    second_heads = lax.ppermute(beyond_heads, EXPERT, OUTWARD)
     act2 = act(kept2, got2, far, 0)
     chip2 = spread_chip(act2)
     got0, got1 = after((got0, got1), act2)
     act0 = act(kept0, got0, near, 0)
     act1 = act(kept1, got1, near, step)
-    (down_near,) = stage([after(w_down, act0, act1)], 0, local)
-    got3 = after(got3, down_near)
+    acts = jnp.concatenate([act0, act1])
+    (down_near,) = stage([after(w_down, acts)], 0, local)
+    got3, beyond_heads = after((got3, beyond_heads), down_near)
     act3 = act(kept3, got3, far, step)
     chip3 = spread_chip(act3)
-    act0, act1 = after((act0, act1), act3)
-    chip0 = spread_chip(act0)
-    chip1 = spread_chip(act1)
+    acts = after(acts, act3)
+    chip0 = spread_chip(acts)
+    second_heads = lax.ppermute(beyond_heads, EXPERT, OUTWARD)
+    far_pieces = [spread(act2, chip2), spread(act3, chip3)]
+    far_first, far_second = down(far_pieces, flags, down_near)
+    in_second = lax.ppermute(far_second, EXPERT, INWARD)
     first_heads, second_heads, beyond_heads = after(
-        (first_heads, second_heads, beyond_heads), act3
+        (first_heads, second_heads, beyond_heads), far_second
     )
     slots = jnp.concatenate(
         [
@@ -628,12 +630,8 @@
         axis=0,
     )
     partial = jnp.dot(slots, w_out, preferred_element_type=jnp.float32).astype(jnp.bfloat16)
-    chip2, chip3 = after((chip2, chip3), partial)
-    far_pieces = [spread(act2, chip2), spread(act3, chip3)]
-    far_first, far_second = down(far_pieces, flags, down_near)
-    in_second = lax.ppermute(far_second, EXPERT, INWARD)
-    chip0, chip1 = after((chip0, chip1), far_first)
-    near_pieces = [spread(act0, chip0), spread(act1, chip1)]
+    acts, chip0 = after((acts, chip0), partial)
+    near_pieces = [spread(acts, chip0)]
     near_own, near_pair = down(near_pieces, flags, down_near)
     far_first = after(far_first, near_own)
     in_first = lax.ppermute(far_first, EXPERT, INWARD)

time: 268 us -> 263 us (0.981)
  the two profiles are of different devices: /device:TPU:18 before, /device:TPU:8 now
where the time goes in v2:
time: 263 us; the launch traced here: 262 us
  waiting for transfers between devices  117 us (44%)
  Pallas kernels  70.7 us (27%)
  starting transfers between devices  49.5 us (19%)
  local copies, waits for them, and re-layouts  12.3 us (5%)
  other arithmetic  7.07 us (3%)
  matrix products  4.01 us (2%)
    ppermute x19, waiting for transfers between devices, flip(): return lax.ppermute(value, axis, [(i, i ^ bit) for i in range(size)])  41 us
    pallas_call x8, Pallas kernels, gate_up(): pl.pallas_call(functools.partial(rows_kernel, parts=len(parts), rows=rows...  25.6 us
    pallas_call x3, Pallas kernels, stage(): pl.pallas_call(functools.partial(stage_kernel, first=first, count=count),...  16.4 us
    ppermute x1, waiting for transfers between devices, layer(): attended = lax.ppermute(mine, (EXPERT, TENSOR), pairs)  15.1 us
    pallas_call x2, Pallas kernels, down(): pl.pallas_call(functools.partial(down_kernel, counts=counts, rows=rows //...  12.4 us
    ppermute x19, starting transfers between devices, flip(): return lax.ppermute(value, axis, [(i, i ^ bit) for i in range(size)])  12.2 us
    ppermute x1, waiting for transfers between devices, layer(): across = lax.ppermute(own, EXPERT, INNER)  12 us
    ppermute x1, waiting for transfers between devices, layer(): second_heads = lax.ppermute(beyond_heads, EXPERT, OUTWARD)  10.8 us
  transfers between devices with their start and end apart: 35, of which 21 were waited for; matrix products, arithmetic and copies ran while one was open for 3% of the time, Pallas kernels for 21%

profile of v2, /device:TPU:8, one launch (start us, length us, event | category | flops | bytes accessed | tf_op | source)
XLA Modules:
  0.0 262.1 jit_solution(4008838534009131610)
XLA Ops:
  6.0 5.3 %stage.3 = (bf16[2,1792,1024]{2,1,0:T(8,128)(2,1)S(1)}, bf16[2,1792,1024]{2,1,0:T(8,128)(2,1)S(1)}) custom-call(bf16[4,1792,1024]{2,1,0:T(8,128)(2,1)} %refs_0_.1, bf16[4,1792,1024]{2,1,0:T(8,128)(2,1)} %refs_1_.1), custom_call_target="tpu_custom_call" | custom-call | bytes 14680064 | tf_op jit(solution)/shard_map/stage/pallas_call | solution.py:356
  11.3 7.5 %collective-permute-done.2.refs_1_ = bf16[128,1920]{1,0:T(8,128)(2,1)S(1)} collective-permute-done((bf16[128,1920]{1,0:T(8,128)(2,1)S(1)}, bf16[128,1920]{1,0:T(8,128)(2,1)S(1)}, u32[]{:S(2)}, u32[]{:S(2)}) %collective-permute-start.2) | collective-permute-done | bytes 491552 | tf_op jit(solution)/shard_map/ppermute | solution.py:561
  18.8 3.1 %gate_up.8 = bf16[2,2,256,512]{3,2,1,0:T(8,128)(2,1)S(1)} custom-call(s32[4]{0:T(128)S(1)} %pad_add_fusion.flags, bf16[128,1920]{1,0:T(8,128)(2,1)S(1)} %concatenate.21.refs_0_, bf16[128,1920]{1,0:T(8,128)(2,1)S(1)} %collective-permute-done.2.refs_1_, bf16[2,1792,1024]{2,1,0:T(8,128)(2,1)S(1)} %get-tuple-element.85.refs_2_.refs_4_, ...), custom_call_target="tpu_custom_call" | custom-call | flops 1879048192 | bytes 7340032 | tf_op jit(solution)/shard_map/gate_up/pallas_call | solution.py:372
  22.0 3.5 %collective-permute-start.3 = (bf16[128,1920]{1,0:T(8,128)(2,1)S(1)}, bf16[128,1920]{1,0:T(8,128)(2,1)S(1)}, u32[]{:S(2)}, u32[]{:S(2)}) collective-permute-start(bf16[128,1920]{1,0:T(8,128)(2,1)S(1)} %concatenate.21.refs_0_), channel_id=1, source_target_pairs={{4,8},{8,4},{5,9},{9,5},{6,10},{10,6},{7,11},{11,7},{20,24},{24,20... | collective-permute-start | bytes 1474568 | tf_op jit(solution)/shard_map/ppermute | solution.py:562
  25.5 12.0 %collective-permute-done.3.refs_0_ = bf16[128,1920]{1,0:T(8,128)(2,1)S(1)} collective-permute-done((bf16[128,1920]{1,0:T(8,128)(2,1)S(1)}, bf16[128,1920]{1,0:T(8,128)(2,1)S(1)}, u32[]{:S(2)}, u32[]{:S(2)}) %collective-permute-start.3) | collective-permute-done | bytes 491552 | tf_op jit(solution)/shard_map/ppermute | solution.py:562
  37.5 3.5 %collective-permute-start.4 = (bf16[128,1920]{1,0:T(8,128)(2,1)S(1)}, bf16[128,1920]{1,0:T(8,128)(2,1)S(1)}, u32[]{:S(2)}, u32[]{:S(2)}) collective-permute-start(bf16[128,1920]{1,0:T(8,128)(2,1)S(1)} %collective-permute-done.2.refs_1_), channel_id=1, source_target_pairs={{4,8},{8,4},{5,9},{9,5},{6,10},{10,6},{7,11},{11,7},{20,24},{24,20... | collective-permute-start | bytes 1474568 | tf_op jit(solution)/shard_map/ppermute | solution.py:583
  45.2 5.8 %stage.4 = (bf16[2,1792,1024]{2,1,0:T(8,128)(2,1)S(1)}, bf16[2,1792,1024]{2,1,0:T(8,128)(2,1)S(1)}) custom-call(bf16[4,1792,1024]{2,1,0:T(8,128)(2,1)} %refs_0_.1, bf16[4,1792,1024]{2,1,0:T(8,128)(2,1)} %refs_1_.1), custom_call_target="tpu_custom_call" | custom-call | bytes 14680064 | tf_op jit(solution)/shard_map/stage/pallas_call | solution.py:356
  52.2 3.9 %gate_up.10 = bf16[2,2,256,512]{3,2,1,0:T(8,128)(2,1)} custom-call(s32[4]{0:T(128)S(1)} %pad_add_fusion.flags, bf16[128,1920]{1,0:T(8,128)(2,1)S(1)} %copy-done.7, bf16[128,1920]{1,0:T(8,128)(2,1)S(1)} %copy-done.11, bf16[2,1792,1024]{2,1,0:T(8,128)(2,1)S(1)} %get-tuple-element.93.refs_2_.refs_4_, bf16[2,1792,1024]{2,1,0:T(8,128)(2,1)S(1)} %get-tuple-element.94.refs_3_.refs_5_), custom_call_target="tpu_custom_call" | custom-call | flops 1879048192 | bytes 7340032 | tf_op jit(solution)/shard_map/gate_up/pallas_call | solution.py:372
  57.7 4.8 %collective-permute-done = bf16[64,640]{1,0:T(8,128)(2,1)S(1)} collective-permute-done((bf16[64,640]{1,0:T(8,128)(2,1)S(1)}, bf16[64,640]{1,0:T(8,128)(2,1)S(1)}, u32[]{:S(2)}, u32[]{:S(2)}) %collective-permute-start) | collective-permute-done | bytes 81952 | tf_op jit(solution)/shard_map/ppermute | solution.py:52
  62.8 7.1 %collective-permute-done.1 = bf16[2,64,640]{2,1,0:T(8,128)(2,1)S(1)} collective-permute-done((bf16[2,64,640]{2,1,0:T(8,128)(2,1)S(1)}, bf16[2,64,640]{2,1,0:T(8,128)(2,1)S(1)}, u32[]{:S(2)}, u32[]{:S(2)}) %collective-permute-start.1) | collective-permute-done | bytes 163872 | tf_op jit(solution)/shard_map/ppermute | solution.py:52
  73.0 3.1 %copy-done.3 = bf16[2,1792,1024]{2,1,0:T(8,128)(2,1)S(1)} copy-done((bf16[2,1792,1024]{2,1,0:T(8,128)(2,1)S(1)}, bf16[2,1792,1024]{2,1,0:T(8,128)(2,1)}, u32[]{:S(2)}) %copy-start.3) | copy-done | bytes 7340056
  83.4 5.7 %collective-permute-start.10 = (bf16[128,1920]{1,0:T(8,128)(2,1)S(1)}, bf16[128,1920]{1,0:T(8,128)(2,1)S(1)}, u32[]{:S(2)}, u32[]{:S(2)}) collective-permute-start(bf16[128,1920]{1,0:T(8,128)(2,1)S(1)} %copy-done.15), channel_id=1, source_target_pairs={{4,0},{8,12},{5,1},{9,13},{6,2},{10,14},{7,3},{11,15},{20,16},{24,... | collective-permute-start | bytes 1474568 | tf_op jit(solution)/shard_map/ppermute | solution.py:584
  91.1 7.2 %attention.1 = bf16[128,2048]{1,0:T(8,128)(2,1)S(1)} custom-call(s32[4]{0:T(128)S(1)} %pad_add_fusion.flags, bf16[128,9216]{1,0:T(8,128)(2,1)S(1)} %copy-done.20, bf16[512,640]{1,0:T(8,128)(2,1)S(1)} %pad_maximum_fusion.1.even_ref, bf16[512,640]{1,0:T(8,128)(2,1)S(1)} %concatenate.25.odd_ref, bf16[16,512,128]{2,1,0:T(8,128)(2,1)S(1)} %copy-done.21), custom_call_target="tpu_custom_call" | custom-call | flops 2550136832 | bytes 2359296 | tf_op jit(solution)/shard_map/attention/pallas_call | solution.py:264
  100.7 10.1 %collective-permute-done.11.refs_3_ = bf16[128,1920]{1,0:T(8,128)(2,1)S(1)} collective-permute-done((bf16[128,1920]{1,0:T(8,128)(2,1)S(1)}, bf16[128,1920]{1,0:T(8,128)(2,1)S(1)}, u32[]{:S(2)}, u32[]{:S(2)}) %collective-permute-start.11) | collective-permute-done | bytes 491552 | tf_op jit(solution)/shard_map/ppermute | solution.py:587
  110.8 3.2 %gate_up.12 = bf16[2,2,256,512]{3,2,1,0:T(8,128)(2,1)S(1)} custom-call(s32[4]{0:T(128)S(1)} %pad_add_fusion.flags, bf16[128,1920]{1,0:T(8,128)(2,1)S(1)} %copy-done.15, bf16[128,1920]{1,0:T(8,128)(2,1)S(1)} %copy-done.17, bf16[128,1920]{1,0:T(8,128)(2,1)S(1)} %collective-permute-done.10.refs_2_, bf16[128,1920]{1,0:T(8,128)(2,1)S(1)} %collective-permute-done.11.refs_3_, ...), custom_call_target="tpu_custom_call" | custom-call | flops 1879048192 | bytes 7340032 | tf_op jit(solution)/shard_map/gate_up/pallas_call | solution.py:372
  114.0 3.1 %gate_up.13.keep_ref = bf16[2,2,256,512]{3,2,1,0:T(8,128)(2,1)S(1)} custom-call(s32[4]{0:T(128)S(1)} %pad_add_fusion.flags, bf16[128,1920]{1,0:T(8,128)(2,1)S(1)} %copy-done.15, bf16[128,1920]{1,0:T(8,128)(2,1)S(1)} %copy-done.17, bf16[128,1920]{1,0:T(8,128)(2,1)S(1)} %collective-permute-done.10.refs_2_, ...), custom_call_target="tpu_custom_call" | custom-call | flops 1879048192 | bytes 7340032 | tf_op jit(solution)/shard_map/gate_up/pallas_call | solution.py:372
  118.3 3.1 %gate_up.14 = bf16[2,2,256,512]{3,2,1,0:T(8,128)(2,1)S(1)} custom-call(s32[4]{0:T(128)S(1)} %pad_add_fusion.flags, bf16[128,1920]{1,0:T(8,128)(2,1)S(1)} %copy-done.15, bf16[128,1920]{1,0:T(8,128)(2,1)S(1)} %copy-done.17, bf16[128,1920]{1,0:T(8,128)(2,1)S(1)} %collective-permute-done.10.refs_2_, bf16[128,1920]{1,0:T(8,128)(2,1)S(1)} %collective-permute-done.11.refs_3_, ...), custom_call_target="tpu_custom_call" | custom-call | flops 1879048192 | bytes 7340032 | tf_op jit(solution)/shard_map/gate_up/pallas_call | solution.py:372
  130.6 3.1 %gate_up.15.keep_ref = bf16[2,2,256,512]{3,2,1,0:T(8,128)(2,1)S(1)} custom-call(s32[4]{0:T(128)S(1)} %pad_add_fusion.flags, bf16[128,1920]{1,0:T(8,128)(2,1)S(1)} %copy-done.15, bf16[128,1920]{1,0:T(8,128)(2,1)S(1)} %copy-done.17, bf16[128,1920]{1,0:T(8,128)(2,1)S(1)} %collective-permute-done.10.refs_2_, ...), custom_call_target="tpu_custom_call" | custom-call | flops 1879048192 | bytes 7340032 | tf_op jit(solution)/shard_map/gate_up/pallas_call | solution.py:372
  136.7 3.3 %collective-permute-done.9 = bf16[128,2048]{1,0:T(8,128)(2,1)S(1)} collective-permute-done((bf16[128,2048]{1,0:T(8,128)(2,1)S(1)}, bf16[128,2048]{1,0:T(8,128)(2,1)S(1)}, u32[]{:S(2)}, u32[]{:S(2)}) %collective-permute-start.9) | collective-permute-done | bytes 524320 | tf_op jit(solution)/shard_map/ppermute | solution.py:597
  141.9 3.5 %collective-permute-start.17 = (bf16[128,2048]{1,0:T(8,128)(2,1)S(1)}, bf16[128,2048]{1,0:T(8,128)(2,1)S(1)}, u32[]{:S(2)}, u32[]{:S(2)}) collective-permute-start(bf16[128,2048]{1,0:T(8,128)(2,1)S(1)} %collective-permute-done.8), channel_id=1, source_target_pairs={{4,8},{8,4},{5,9},{9,5},{6,10},{10,6},{7,11},{11,7},{20,24},{24,20... | collective-permute-start | bytes 1572872 | tf_op jit(solution)/shard_map/ppermute | solution.py:602
  148.6 4.6 %collective-permute-done.18.got_ref = bf16[2,2,256,256]{3,2,1,0:T(8,128)(2,1)S(1)} collective-permute-done((bf16[2,2,256,256]{3,2,1,0:T(8,128)(2,1)S(1)}, bf16[2,2,256,256]{3,2,1,0:T(8,128)(2,1)S(1)}, u32[]{:S(2)}, u32[]{:S(2)}) %collective-permute-start.18) | collective-permute-done | bytes 524320 | tf_op jit(solution)/shard_map/ppermute | solution.py:52
  153.2 11.2 %collective-permute-done.19.got_ref = bf16[2,2,256,256]{3,2,1,0:T(8,128)(2,1)S(1)} collective-permute-done((bf16[2,2,256,256]{3,2,1,0:T(8,128)(2,1)S(1)}, bf16[2,2,256,256]{3,2,1,0:T(8,128)(2,1)S(1)}, u32[]{:S(2)}, u32[]{:S(2)}) %collective-permute-start.19) | collective-permute-done | bytes 524320 | tf_op jit(solution)/shard_map/ppermute | solution.py:52
  166.4 5.3 %stage.5.refs_4_.refs_2_ = bf16[4,1024,1792]{2,1,0:T(8,128)(2,1)S(1)} custom-call(bf16[4,1024,1792]{2,1,0:T(8,128)(2,1)} %refs_0_.2), custom_call_target="tpu_custom_call" | custom-call | bytes 14680064 | tf_op jit(solution)/shard_map/stage/pallas_call | solution.py:356
  171.7 3.9 %collective-permute-done.16.got_ref = bf16[2,2,256,256]{3,2,1,0:T(8,128)(2,1)S(1)} collective-permute-done((bf16[2,2,256,256]{3,2,1,0:T(8,128)(2,1)S(1)}, bf16[2,2,256,256]{3,2,1,0:T(8,128)(2,1)S(1)}, u32[]{:S(2)}, u32[]{:S(2)}) %collective-permute-start.16) | collective-permute-done | bytes 524320 | tf_op jit(solution)/shard_map/ppermute | solution.py:52
  181.4 4.0 %collective-permute-done.23 = bf16[2,256,256]{2,1,0:T(8,128)(2,1)S(1)} collective-permute-done((bf16[2,256,256]{2,1,0:T(8,128)(2,1)S(1)}, bf16[2,256,256]{2,1,0:T(8,128)(2,1)S(1)}, u32[]{:S(2)}, u32[]{:S(2)}) %collective-permute-start.23) | collective-permute-done | bytes 262176 | tf_op jit(solution)/shard_map/ppermute | solution.py:52
  190.0 6.2 %down.2 = (bf16[128,1792]{1,0:T(8,128)(2,1)S(1)}, bf16[128,1792]{1,0:T(8,128)(2,1)S(1)}) custom-call(s32[4]{0:T(128)S(1)} %pad_add_fusion.flags, bf16[2,2,256,256]{3,2,1,0:T(8,128)(2,1)S(1)} %pad_maximum_fusion.3.refs_0_, bf16[2,2,256,256]{3,2,1,0:T(8,128)(2,1)S(1)} %collective-permute-done.22.refs_1_, ...), custom_call_target="tpu_custom_call" | custom-call | flops 3758096384 | bytes 14680064 | tf_op jit(solution)/shard_map/down/pallas_call | solution.py:438
  199.4 10.8 %collective-permute-done.20 = bf16[128,2048]{1,0:T(8,128)(2,1)S(1)} collective-permute-done((bf16[128,2048]{1,0:T(8,128)(2,1)S(1)}, bf16[128,2048]{1,0:T(8,128)(2,1)S(1)}, u32[]{:S(2)}, u32[]{:S(2)}) %collective-permute-start.20) | collective-permute-done | bytes 524320 | tf_op jit(solution)/shard_map/ppermute | solution.py:616
  210.3 4.0 %convolution_convert_fusion = bf16[512,1792]{1,0:T(8,128)(2,1)S(1)} fusion(bf16[2048,1792]{1,0:T(8,128)(2,1)S(1)} %bitcast.39, bf16[128,2048]{1,0:T(8,128)(2,1)S(1)} %get-tuple-element.154, bf16[128,2048]{1,0:T(8,128)(2,1)S(1)} %get-tuple-element.155, bf16[128,2048]{1,0:T(8,128)(2,1)S(1)} %collective-permute-done.8, bf16[128,2048]{1,0:T(8,128)(2,1)S(1)} %copy-done.23), kind=kOutput, calls=%fused_computation.1 | convolution fusion | flops 3767402496 | bytes 11272192 | tf_op jit(solution)/shard_map/dot_general | solution.py:632
  215.3 3.5 %collective-permute-start.33 = (bf16[128,1792]{1,0:T(8,128)(2,1)S(1)}, bf16[128,1792]{1,0:T(8,128)(2,1)S(1)}, u32[]{:S(2)}, u32[]{:S(2)}) collective-permute-start(bf16[128,1792]{1,0:T(8,128)(2,1)S(1)} %add_convert_fusion.3), channel_id=1, source_target_pairs={{4,8},{8,4},{5,9},{9,5},{6,10},{10,6},{7,11},{11,7},{20,24},{24,20... | collective-permute-start | bytes 1376264 | tf_op jit(solution)/shard_map/ppermute | solution.py:638
  220.8 6.2 %down.3 = (bf16[128,1792]{1,0:T(8,128)(2,1)S(1)}, bf16[128,1792]{1,0:T(8,128)(2,1)S(1)}) custom-call(s32[4]{0:T(128)S(1)} %pad_add_fusion.flags, bf16[2,4,256,256]{3,2,1,0:T(8,128)(2,1)S(1)} %pad_maximum_fusion.refs_0_, bf16[2,4,256,256]{3,2,1,0:T(8,128)(2,1)S(1)} %collective-permute-done.29.refs_1_, bf16[4,1024,1792]{2,1,0:T(8,128)(2,1)S(1)} %stage.5.refs_4_.refs_2_), custom_call_target="tpu_custom_call" | custom-call | flops 3758096384 | bytes 14680064 | tf_op jit(solution)/shard_map/down/pallas_call | solution.py:438
  233.6 8.7 %collective-permute-done.30 = bf16[128,1792]{1,0:T(8,128)(2,1)S(1)} collective-permute-done((bf16[128,1792]{1,0:T(8,128)(2,1)S(1)}, bf16[128,1792]{1,0:T(8,128)(2,1)S(1)}, u32[]{:S(2)}, u32[]{:S(2)}) %collective-permute-start.30) | collective-permute-done | bytes 458784 | tf_op jit(solution)/shard_map/ppermute | solution.py:637
  245.3 15.1 %collective-permute-done.27 = bf16[128,1792]{1,0:T(8,128)(2,1)S(1)} collective-permute-done((bf16[128,1792]{1,0:T(8,128)(2,1)S(1)}, bf16[128,1792]{1,0:T(8,128)(2,1)S(1)}, u32[]{:S(2)}, u32[]{:S(2)}) %collective-permute-start.27) | collective-permute-done | bytes 458784 | tf_op jit(solution)/shard_map/ppermute | solution.py:656
  (185 shorter events, 75.1 us)
Async XLA Ops:
  5.8 13.0 %collective-permute-start.2 = (bf16[128,1920]{1,0:T(8,128)(2,1)S(1)}, bf16[128,1920]{1,0:T(8,128)(2,1)S(1)}, u32[]{:S(2)}, u32[]{:S(2)}) collective-permute-start(bf16[128,1920]{1,0:T(8,128)(2,1)S(1)} %concatenate.21.refs_0_), channel_id=1, source_target_pairs={{0,4},{4,0},{8,12},{12,8},{1,5},{5,1},{9,13},{13,9},{2,6},{6,2},{1... | collective-permute-start | bytes 1474568 | tf_op jit(solution)/shard_map/ppermute | solution.py:561
  21.9 22.1 %collective-permute-start.5 = (bf16[2,2,256,512]{3,2,1,0:T(8,128)(2,1)S(1)}, bf16[2,2,256,512]{3,2,1,0:T(8,128)(2,1)S(1)}, u32[]{:S(2)}, u32[]{:S(2)}) collective-permute-start(bf16[2,2,256,512]{3,2,1,0:T(8,128)(2,1)S(1)} %gate_up.8), channel_id=1, source_target_pairs={{0,1},{1,0},{2,3},{3,2},{4,5},{5,4},{6,7},{7,6},{8,9},{9,8},{10,11... | collective-permute-start | bytes 3145736 | tf_op jit(solution)/shard_map/ppermute | solution.py:52
  22.0 15.5 %collective-permute-start.3 = (bf16[128,1920]{1,0:T(8,128)(2,1)S(1)}, bf16[128,1920]{1,0:T(8,128)(2,1)S(1)}, u32[]{:S(2)}, u32[]{:S(2)}) collective-permute-start(bf16[128,1920]{1,0:T(8,128)(2,1)S(1)} %concatenate.21.refs_0_), channel_id=1, source_target_pairs={{4,8},{8,4},{5,9},{9,5},{6,10},{10,6},{7,11},{11,7},{20,24},{24,20... | collective-permute-start | bytes 1474568 | tf_op jit(solution)/shard_map/ppermute | solution.py:562
  37.5 14.6 %collective-permute-start.4 = (bf16[128,1920]{1,0:T(8,128)(2,1)S(1)}, bf16[128,1920]{1,0:T(8,128)(2,1)S(1)}, u32[]{:S(2)}, u32[]{:S(2)}) collective-permute-start(bf16[128,1920]{1,0:T(8,128)(2,1)S(1)} %collective-permute-done.2.refs_1_), channel_id=1, source_target_pairs={{4,8},{8,4},{5,9},{9,5},{6,10},{10,6},{7,11},{11,7},{20,24},{24,20... | collective-permute-start | bytes 1474568 | tf_op jit(solution)/shard_map/ppermute | solution.py:583
  57.4 23.8 %collective-permute-start.6 = (bf16[2,2,256,512]{3,2,1,0:T(8,128)(2,1)}, bf16[2,2,256,512]{3,2,1,0:T(8,128)(2,1)}, u32[]{:S(2)}, u32[]{:S(2)}) collective-permute-start(bf16[2,2,256,512]{3,2,1,0:T(8,128)(2,1)} %gate_up.10), channel_id=1, source_target_pairs={{0,1},{1,0},{2,3},{3,2},{4,5},{5,4},{6,7},{7,6},{8,9},{9,8},{10,11... | collective-permute-start | bytes 3145736 | tf_op jit(solution)/shard_map/ppermute | solution.py:52
  57.6 4.9 %collective-permute-start = (bf16[64,640]{1,0:T(8,128)(2,1)S(1)}, bf16[64,640]{1,0:T(8,128)(2,1)S(1)}, u32[]{:S(2)}, u32[]{:S(2)}) collective-permute-start(bf16[64,640]{1,0:T(8,128)(2,1)S(1)} %slice_select_fusion), channel_id=1, source_target_pairs={{0,4},{4,0},{8,12},{12,8},{1,5},{5,1},{9,13},{13,9},{2,6},{6,2},{1... | collective-permute-start | bytes 245768 | tf_op jit(solution)/shard_map/ppermute | solution.py:52
  62.6 7.3 %collective-permute-start.1 = (bf16[2,64,640]{2,1,0:T(8,128)(2,1)S(1)}, bf16[2,64,640]{2,1,0:T(8,128)(2,1)S(1)}, u32[]{:S(2)}, u32[]{:S(2)}) collective-permute-start(bf16[2,64,640]{2,1,0:T(8,128)(2,1)S(1)} %pad_maximum_fusion.7), channel_id=1, source_target_pairs={{0,8},{4,12},{8,0},{12,4},{1,9},{5,13},{9,1},{13,5},{2,10},{6,14},... | collective-permute-start | bytes 491528 | tf_op jit(solution)/shard_map/ppermute | solution.py:52
  83.2 7.2 %collective-permute-start.7 = (bf16[3,64,640]{2,1,0:T(8,128)(2,1)S(1)}, bf16[3,64,640]{2,1,0:T(8,128)(2,1)S(1)}, u32[]{:S(2)}, u32[]{:S(2)}) collective-permute-start(bf16[3,64,640]{2,1,0:T(8,128)(2,1)S(1)} %pad_maximum_fusion.5), channel_id=1, source_target_pairs={{0,1},{1,0},{2,3},{3,2},{4,5},{5,4},{6,7},{7,6},{8,9},{9,8},{10,11... | collective-permute-start | bytes 737288 | tf_op jit(solution)/shard_map/ppermute | solution.py:52
  83.4 17.3 %collective-permute-start.10 = (bf16[128,1920]{1,0:T(8,128)(2,1)S(1)}, bf16[128,1920]{1,0:T(8,128)(2,1)S(1)}, u32[]{:S(2)}, u32[]{:S(2)}) collective-permute-start(bf16[128,1920]{1,0:T(8,128)(2,1)S(1)} %copy-done.15), channel_id=1, source_target_pairs={{4,0},{8,12},{5,1},{9,13},{6,2},{10,14},{7,3},{11,15},{20,16},{24,... | collective-permute-start | bytes 1474568 | tf_op jit(solution)/shard_map/ppermute | solution.py:584
  89.1 21.6 %collective-permute-start.11 = (bf16[128,1920]{1,0:T(8,128)(2,1)S(1)}, bf16[128,1920]{1,0:T(8,128)(2,1)S(1)}, u32[]{:S(2)}, u32[]{:S(2)}) collective-permute-start(bf16[128,1920]{1,0:T(8,128)(2,1)S(1)} %copy-done.17), channel_id=1, source_target_pairs={{4,0},{8,12},{5,1},{9,13},{6,2},{10,14},{7,3},{11,15},{20,16},{24,... | collective-permute-start | bytes 1474568 | tf_op jit(solution)/shard_map/ppermute | solution.py:587
  121.4 7.7 %collective-permute-start.14 = (bf16[2,2,256,512]{3,2,1,0:T(8,128)(2,1)S(1)}, bf16[2,2,256,512]{3,2,1,0:T(8,128)(2,1)S(1)}, u32[]{:S(2)}, u32[]{:S(2)}) collective-permute-start(bf16[2,2,256,512]{3,2,1,0:T(8,128)(2,1)S(1)} %gate_up.14), channel_id=1, source_target_pairs={{0,1},{1,0},{2,3},{3,2},{4,5},{5,4},{6,7},{7,6},{8,9},{9,8},{10,11... | collective-permute-start | bytes 3145736 | tf_op jit(solution)/shard_map/ppermute | solution.py:52
  122.0 14.7 %collective-permute-start.8 = (bf16[128,2048]{1,0:T(8,128)(2,1)S(1)}, bf16[128,2048]{1,0:T(8,128)(2,1)S(1)}, u32[]{:S(2)}, u32[]{:S(2)}) collective-permute-start(bf16[128,2048]{1,0:T(8,128)(2,1)S(1)} %attention.1), channel_id=1, source_target_pairs={{0,4},{4,0},{8,12},{12,8},{1,5},{5,1},{9,13},{13,9},{2,6},{6,2},{1... | collective-permute-start | bytes 1572872 | tf_op jit(solution)/shard_map/ppermute | solution.py:596
  124.5 15.5 %collective-permute-start.9 = (bf16[128,2048]{1,0:T(8,128)(2,1)S(1)}, bf16[128,2048]{1,0:T(8,128)(2,1)S(1)}, u32[]{:S(2)}, u32[]{:S(2)}) collective-permute-start(bf16[128,2048]{1,0:T(8,128)(2,1)S(1)} %attention.1), channel_id=1, source_target_pairs={{4,8},{8,4},{5,9},{9,5},{6,10},{10,6},{7,11},{11,7},{20,24},{24,20... | collective-permute-start | bytes 1572872 | tf_op jit(solution)/shard_map/ppermute | solution.py:597
  127.1 14.9 %collective-permute-start.13 = (bf16[2,2,256,256]{3,2,1,0:T(8,128)(2,1)S(1)}, bf16[2,2,256,256]{3,2,1,0:T(8,128)(2,1)S(1)}, u32[]{:S(2)}, u32[]{:S(2)}) collective-permute-start(bf16[2,2,256,256]{3,2,1,0:T(8,128)(2,1)S(1)} %get-tuple-element.111), channel_id=1, source_target_pairs={{0,2},{1,3},{2,0},{3,1},{4,6},{5,7},{6,4},{7,5},{8,10},{9,11},{10,... | collective-permute-start | bytes 1572872 | tf_op jit(solution)/shard_map/ppermute | solution.py:52
  128.6 24.5 %collective-permute-start.18 = (bf16[2,2,256,256]{3,2,1,0:T(8,128)(2,1)S(1)}, bf16[2,2,256,256]{3,2,1,0:T(8,128)(2,1)S(1)}, u32[]{:S(2)}, u32[]{:S(2)}) collective-permute-start(bf16[2,2,256,256]{3,2,1,0:T(8,128)(2,1)S(1)} %copy-done.25), channel_id=1, source_target_pairs={{0,2},{1,3},{2,0},{3,1},{4,6},{5,7},{6,4},{7,5},{8,10},{9,11},{10,... | collective-permute-start | bytes 1572872 | tf_op jit(solution)/shard_map/ppermute | solution.py:52
  129.2 35.2 %collective-permute-start.19 = (bf16[2,2,256,256]{3,2,1,0:T(8,128)(2,1)S(1)}, bf16[2,2,256,256]{3,2,1,0:T(8,128)(2,1)S(1)}, u32[]{:S(2)}, u32[]{:S(2)}) collective-permute-start(bf16[2,2,256,256]{3,2,1,0:T(8,128)(2,1)S(1)} %get-tuple-element.99), channel_id=1, source_target_pairs={{0,2},{1,3},{2,0},{3,1},{4,6},{5,7},{6,4},{7,5},{8,10},{9,11},{10,... | collective-permute-start | bytes 1572872 | tf_op jit(solution)/shard_map/ppermute | solution.py:52
  141.9 29.8 %collective-permute-start.17 = (bf16[128,2048]{1,0:T(8,128)(2,1)S(1)}, bf16[128,2048]{1,0:T(8,128)(2,1)S(1)}, u32[]{:S(2)}, u32[]{:S(2)}) collective-permute-start(bf16[128,2048]{1,0:T(8,128)(2,1)S(1)} %collective-permute-done.8), channel_id=1, source_target_pairs={{4,8},{8,4},{5,9},{9,5},{6,10},{10,6},{7,11},{11,7},{20,24},{24,20... | collective-permute-start | bytes 1572872 | tf_op jit(solution)/shard_map/ppermute | solution.py:602
  145.4 30.2 %collective-permute-start.16 = (bf16[2,2,256,256]{3,2,1,0:T(8,128)(2,1)S(1)}, bf16[2,2,256,256]{3,2,1,0:T(8,128)(2,1)S(1)}, u32[]{:S(2)}, u32[]{:S(2)}) collective-permute-start(bf16[2,2,256,256]{3,2,1,0:T(8,128)(2,1)S(1)} %get-tuple-element.120), channel_id=1, source_target_pairs={{0,2},{1,3},{2,0},{3,1},{4,6},{5,7},{6,4},{7,5},{8,10},{9,11},{10,... | collective-permute-start | bytes 1572872 | tf_op jit(solution)/shard_map/ppermute | solution.py:52
  147.9 33.3 %collective-permute-start.21 = (bf16[2,256,256]{2,1,0:T(8,128)(2,1)S(1)}, bf16[2,256,256]{2,1,0:T(8,128)(2,1)S(1)}, u32[]{:S(2)}, u32[]{:S(2)}) collective-permute-start(bf16[2,256,256]{2,1,0:T(8,128)(2,1)S(1)} %activate.4), channel_id=1, source_target_pairs={{0,2},{1,3},{2,0},{3,1},{4,6},{5,7},{6,4},{7,5},{8,10},{9,11},{10,... | collective-permute-start | bytes 786440 | tf_op jit(solution)/shard_map/ppermute | solution.py:52
  176.6 8.8 %collective-permute-start.23 = (bf16[2,256,256]{2,1,0:T(8,128)(2,1)S(1)}, bf16[2,256,256]{2,1,0:T(8,128)(2,1)S(1)}, u32[]{:S(2)}, u32[]{:S(2)}) collective-permute-start(bf16[2,256,256]{2,1,0:T(8,128)(2,1)S(1)} %activate.7), channel_id=1, source_target_pairs={{0,2},{1,3},{2,0},{3,1},{4,6},{5,7},{6,4},{7,5},{8,10},{9,11},{10,... | collective-permute-start | bytes 786440 | tf_op jit(solution)/shard_map/ppermute | solution.py:52
  181.3 8.7 %collective-permute-start.22 = (bf16[2,2,256,256]{3,2,1,0:T(8,128)(2,1)S(1)}, bf16[2,2,256,256]{3,2,1,0:T(8,128)(2,1)S(1)}, u32[]{:S(2)}, u32[]{:S(2)}) collective-permute-start(bf16[2,2,256,256]{3,2,1,0:T(8,128)(2,1)S(1)} %pad_maximum_fusion.3.refs_0_), channel_id=1, source_target_pairs={{0,1},{1,0},{2,3},{3,2},{4,5},{5,4},{6,7},{7,6},{8,9},{9,8},{10,11... | collective-permute-start | bytes 1572872 | tf_op jit(solution)/shard_map/ppermute | solution.py:52
  185.6 13.9 %collective-permute-start.15 = (bf16[128,2048]{1,0:T(8,128)(2,1)S(1)}, bf16[128,2048]{1,0:T(8,128)(2,1)S(1)}, u32[]{:S(2)}, u32[]{:S(2)}) collective-permute-start(bf16[128,2048]{1,0:T(8,128)(2,1)S(1)} %collective-permute-done.9), channel_id=1, source_target_pairs={{4,0},{8,12},{5,1},{9,13},{6,2},{10,14},{7,3},{11,15},{20,16},{24,... | collective-permute-start | bytes 1572872 | tf_op jit(solution)/shard_map/ppermute | solution.py:603
  187.2 23.0 %collective-permute-start.20 = (bf16[128,2048]{1,0:T(8,128)(2,1)S(1)}, bf16[128,2048]{1,0:T(8,128)(2,1)S(1)}, u32[]{:S(2)}, u32[]{:S(2)}) collective-permute-start(bf16[128,2048]{1,0:T(8,128)(2,1)S(1)} %collective-permute-done.17), channel_id=1, source_target_pairs={{4,0},{8,12},{5,1},{9,13},{6,2},{10,14},{7,3},{11,15},{20,16},{24,... | collective-permute-start | bytes 1572872 | tf_op jit(solution)/shard_map/ppermute | solution.py:616
  188.5 26.0 %collective-permute-start.28 = (bf16[4,256,256]{2,1,0:T(8,128)(2,1)S(1)}, bf16[4,256,256]{2,1,0:T(8,128)(2,1)S(1)}, u32[]{:S(2)}, u32[]{:S(2)}) collective-permute-start(bf16[4,256,256]{2,1,0:T(8,128)(2,1)S(1)} %pad_maximum_fusion.2), channel_id=1, source_target_pairs={{0,2},{1,3},{2,0},{3,1},{4,6},{5,7},{6,4},{7,5},{8,10},{9,11},{10,... | collective-permute-start | bytes 1572872 | tf_op jit(solution)/shard_map/ppermute | solution.py:52
  196.3 19.0 %collective-permute-start.32 = (bf16[128,1792]{1,0:T(8,128)(2,1)S(1)}, bf16[128,1792]{1,0:T(8,128)(2,1)S(1)}, u32[]{:S(2)}, u32[]{:S(2)}) collective-permute-start(bf16[128,1792]{1,0:T(8,128)(2,1)S(1)} %get-tuple-element.138), channel_id=1, source_target_pairs={{0,4},{12,8},{1,5},{13,9},{2,6},{14,10},{3,7},{15,11},{16,20},{28,... | collective-permute-start | bytes 1376264 | tf_op jit(solution)/shard_map/ppermute | solution.py:619
  214.7 6.1 %collective-permute-start.29 = (bf16[2,4,256,256]{3,2,1,0:T(8,128)(2,1)S(1)}, bf16[2,4,256,256]{3,2,1,0:T(8,128)(2,1)S(1)}, u32[]{:S(2)}, u32[]{:S(2)}) collective-permute-start(bf16[2,4,256,256]{3,2,1,0:T(8,128)(2,1)S(1)} %pad_maximum_fusion.refs_0_), channel_id=1, source_target_pairs={{0,1},{1,0},{2,3},{3,2},{4,5},{5,4},{6,7},{7,6},{8,9},{9,8},{10,11... | collective-permute-start | bytes 3145736 | tf_op jit(solution)/shard_map/ppermute | solution.py:52
  215.3 14.3 %collective-permute-start.33 = (bf16[128,1792]{1,0:T(8,128)(2,1)S(1)}, bf16[128,1792]{1,0:T(8,128)(2,1)S(1)}, u32[]{:S(2)}, u32[]{:S(2)}) collective-permute-start(bf16[128,1792]{1,0:T(8,128)(2,1)S(1)} %add_convert_fusion.3), channel_id=1, source_target_pairs={{4,8},{8,4},{5,9},{9,5},{6,10},{10,6},{7,11},{11,7},{20,24},{24,20... | collective-permute-start | bytes 1376264 | tf_op jit(solution)/shard_map/ppermute | solution.py:638
  219.2 12.2 %collective-permute-start.26 = (bf16[128,1792]{1,0:T(8,128)(2,1)S(1)}, bf16[128,1792]{1,0:T(8,128)(2,1)S(1)}, u32[]{:S(2)}, u32[]{:S(2)}) collective-permute-start(bf16[128,1792]{1,0:T(8,128)(2,1)S(1)} %broadcast_select_fusion.3), channel_id=1, source_target_pairs={{0,2},{1,3},{2,0},{3,1},{4,6},{5,7},{6,4},{7,5},{8,10},{9,11},{10,... | collective-permute-start | bytes 1376264 | tf_op jit(solution)/shard_map/ppermute | solution.py:52
  226.9 15.3 %collective-permute-start.30 = (bf16[128,1792]{1,0:T(8,128)(2,1)S(1)}, bf16[128,1792]{1,0:T(8,128)(2,1)S(1)}, u32[]{:S(2)}, u32[]{:S(2)}) collective-permute-start(bf16[128,1792]{1,0:T(8,128)(2,1)S(1)} %get-tuple-element.147), channel_id=1, source_target_pairs={{0,4},{12,8},{1,5},{13,9},{2,6},{14,10},{3,7},{15,11},{16,20},{28,... | collective-permute-start | bytes 1376264 | tf_op jit(solution)/shard_map/ppermute | solution.py:637
  229.8 30.6 %collective-permute-start.34 = (bf16[128,1792]{1,0:T(8,128)(2,1)S(1)}, bf16[128,1792]{1,0:T(8,128)(2,1)S(1)}, u32[]{:S(2)}, u32[]{:S(2)}) collective-permute-start(bf16[128,1792]{1,0:T(8,128)(2,1)S(1)} %add_convert_fusion.2), channel_id=1, source_target_pairs={{0,4},{4,0},{8,12},{12,8},{1,5},{5,1},{9,13},{13,9},{2,6},{6,2},{1... | collective-permute-start | bytes 1376264 | tf_op jit(solution)/shard_map/ppermute | solution.py:640
  231.6 28.7 %collective-permute-start.27 = (bf16[128,1792]{1,0:T(8,128)(2,1)S(1)}, bf16[128,1792]{1,0:T(8,128)(2,1)S(1)}, u32[]{:S(2)}, u32[]{:S(2)}) collective-permute-start(bf16[128,1792]{1,0:T(8,128)(2,1)S(1)} %add_convert_fusion.5), channel_id=1, source_target_pairs={{0,0},{1,8},{2,4},{3,12},{4,5},{5,9},{6,1},{7,13},{8,10},{9,6},{10... | collective-permute-start | bytes 1376264 | tf_op jit(solution)/shard_map/ppermute | solution.py:656
  242.3 18.0 %collective-permute-start.31 = (bf16[128,1792]{1,0:T(8,128)(2,1)S(1)}, bf16[128,1792]{1,0:T(8,128)(2,1)S(1)}, u32[]{:S(2)}, u32[]{:S(2)}) collective-permute-start(bf16[128,1792]{1,0:T(8,128)(2,1)S(1)} %add_convert_fusion.4), channel_id=1, source_target_pairs={{4,8},{8,4},{5,9},{9,5},{6,10},{10,6},{7,11},{11,7},{20,24},{24,20... | collective-permute-start | bytes 1376264 | tf_op jit(solution)/shard_map/ppermute | solution.py:639
  (43 other events, 615.3 us)
